TPU v7x, 256 devices: a whole 4x4x8 slice. The times are simulated.
256 devices in a mesh: cell: 8 (over y, z_hi), gene: 32 (over x, z_lo, core).
Axes of the slice: x: 4, y: 4, z: 8 (z_hi: 2, z_lo: 4; z = z_hi * 4 + z_lo), core: 2. Of those that a mesh axis runs over, the one named last changes fastest.
Arguments:
- blocks: bfloat16 [12288, 256, 256], P(('cell', 'gene')), may hold values from 0 to 255, as said below
- block_rows: int32 [12288], P(('cell', 'gene')), may hold values from 0 to 15, as said below
- block_cols: int32 [12288], P(('cell', 'gene')), may hold values from 0 to 3, as said below
- block_count: int32 [256], P(('cell', 'gene')), may hold values from 2 to 48, as said below
- cell_factor: float32 [32768, 128], P(('cell', 'gene')), as said below
- gene_factor: float32 [32768, 128], P('gene'), as said below
Outputs:
- cell_new: float32 [32768, 128], P(('cell', 'gene'))
- gene_new: float32 [32768, 128], P('gene')
Inputs may be any that keep to these rules, and one draw needn't show every extreme that they name: `blocks`: counts are whole numbers. `block_rows`: within one device the live slots and the padding slots name distinct block positions. `block_cols`: within one device the live slots and the padding slots name distinct block positions. `block_count`: some device has all 48 slots live. `cell_factor`: positive entries. `gene_factor`: positive entries.
All inputs are finite; a program needn't handle non-finite values.
Results may differ from a plain program's by a relative error of at most 0.00084.
Values may be sent and summed in bfloat16 or wider, within the bound.
No kernel may reach another device: no remote copies, remote signals or barrier semaphores. Data moves between devices by JAX's collectives and lax.ppermute only.
A program may use at most 64 MiB of HBM per device.

v0:
```python
import functools

import jax
import jax.numpy as jnp
from jax import lax
from jax.sharding import Mesh
from jax.sharding import PartitionSpec as P

GENE = ("gene_0", "gene_1", "gene_2")
CELL_GENE = ("cell_0", "cell_1", "gene_0", "gene_1", "gene_2")
CELL = ("cell_0", "cell_1")


def sent_to_all(shard, axis):
    count = lax.axis_size(axis)
    return lax.all_to_all(
        jnp.broadcast_to(shard[None], (count, *shard.shape)), axis, 0, 0, tiled=True
    )


def over_copies(shard, axis):
    everything = sent_to_all(shard, axis)
    return jnp.sum(everything, axis=0)


def joined_along(blocks, dim):
    dims = list(blocks.shape[1:])
    dims[dim] *= blocks.shape[0]
    return jnp.moveaxis(blocks, 0, dim).reshape(dims)


def collect(shard, axis, dim):
    return joined_along(sent_to_all(shard, axis), dim)


def cut_along(shard, dim, count):
    before, after = (shard.shape[:dim], shard.shape[dim + 1 :])
    return jnp.moveaxis(shard.reshape(*before, count, -1, *after), dim, 0)


def sent_and_summed(shard, axis, dim):
    blocks = cut_along(shard, dim, lax.axis_size(axis))
    arrived = lax.all_to_all(blocks, axis, split_axis=0, concat_axis=0, tiled=True)
    return arrived.sum(axis=0)


def by_axis(shard, axes):
    return functools.reduce(lax.psum, axes, shard)


def block_ratio(blocks, row_tiles, col_tiles, live):
    model = jnp.einsum("nir,njr->nij", row_tiles, col_tiles, preferred_element_type=jnp.float32)
    return (blocks.astype(jnp.float32) / model * live[:, None, None]).astype(jnp.bfloat16)


def on_device(blocks, block_rows, block_cols, block_count, cell_factor, gene_factor):
    slots = blocks.shape[0]
    width = blocks.shape[1]
    rank = cell_factor.shape[1]
    gene_len = gene_factor.shape[0]
    live = (jnp.arange(slots, dtype=jnp.int32) < block_count[0]).astype(jnp.float32)
    gene_bf = gene_factor.astype(jnp.bfloat16)
    gene_tiles = gene_bf.reshape(-1, width, rank)[block_cols]
    gene_totals = over_copies(jnp.sum(gene_factor, 0), GENE)
    cell_bf = collect(cell_factor.astype(jnp.bfloat16), GENE, 0)
    row_count = cell_bf.shape[0] // width
    row_pick = (block_rows[None, :] == jnp.arange(row_count, dtype=jnp.int32)[:, None]).astype(
        jnp.float32
    )
    col_pick = (
        block_cols[None, :] == jnp.arange(gene_len // width, dtype=jnp.int32)[:, None]
    ).astype(jnp.float32)
    row_tiles = cell_bf.reshape(row_count, width, rank)[block_rows]
    ratio = block_ratio(blocks, row_tiles, gene_tiles, live)
    terms = jnp.einsum("nij,njr->nir", ratio, gene_tiles, preferred_element_type=jnp.float32)
    numer = jnp.einsum("bn,nir->bir", row_pick, terms, precision=lax.Precision.HIGHEST).reshape(
        -1, rank
    )
    share = sent_and_summed(numer, GENE, 0)
    cell_new = cell_factor * share / gene_totals
    new_bf = collect(cell_new.astype(jnp.bfloat16), GENE, 0)
    cell_sums = by_axis(jnp.sum(cell_new, 0), CELL_GENE)
    new_tiles = new_bf.reshape(row_count, width, rank)[block_rows]
    ratio_next = block_ratio(blocks, new_tiles, gene_tiles, live)
    terms_next = jnp.einsum(
        "nij,nir->njr", ratio_next, new_tiles, preferred_element_type=jnp.float32
    )
    numer_gene = jnp.einsum(
        "bn,njr->bjr", col_pick, terms_next, precision=lax.Precision.HIGHEST
    ).reshape(-1, rank)
    portion = sent_and_summed(numer_gene, CELL, 0)
    own_genes = portion.shape[0]
    mine = lax.dynamic_slice_in_dim(gene_factor, lax.axis_index(CELL) * own_genes, own_genes, 0)
    gene_new = collect(mine * portion / cell_sums, CELL, 0)
    return (cell_new, gene_new)


def solution(mesh):
    torus = Mesh(
        mesh.devices.reshape(4, 2, 4, 4, 2), ("cell_0", "cell_1", "gene_0", "gene_1", "gene_2")
    )
    return jax.shard_map(
        on_device,
        mesh=torus,
        in_specs=(
            P(CELL_GENE, None, None),
            P(CELL_GENE),
            P(CELL_GENE),
            P(CELL_GENE),
            P(CELL_GENE, None),
            P(GENE, None),
        ),
        out_specs=(P(CELL_GENE, None), P(GENE, None)),
        check_vma=False,
    )
```

profile of v0, /device:TPU:1, one launch (start us, length us, event | category | flops | bytes accessed | tf_op | source)
XLA Modules:
  0.0 257.2 jit_solution(14518441419085385588)
XLA Ops:
  0.6 0.0 copy-start.4
  0.6 0.0 copy-start
  0.6 0.9 convert_element_type.29
  1.6 1.2 broadcast_in_dim.12
  2.8 10.0 %all-to-all-start = ((bf16[32,128,128]{2,1,0:T(8,128)(2,1)}), bf16[32,128,128]{2,1,0:T(8,128)(2,1)S(1)}, u32[]{:S(2)}, u32[]{:S(2)}) async-start(bf16[32,128,128]{2,1,0:T(8,128)(2,1)} %broadcast_in_dim.12), calls=%async_computation | async-start | bytes 2097152 | tf_op jit(solution)/shard_map/all_to_all | solution.py:16
  13.5 0.0 copy-done.4
  13.5 0.0 copy-done
  13.5 0.1 fusion.23
  13.7 0.0 copy-start.3
  13.7 2.8 %gather_fusion.1 = bf16[48,256,128]{2,1,0:T(8,128)(2,1)} fusion(bf16[4,256,128]{2,1,0:T(8,128)(2,1)S(1)} %bitcast.21, s32[1024]{0:T(1024)S(1)} %pad_clamp_fusion), kind=kCustom, calls=%fused_computation.1 | custom fusion | bytes 6291648 | tf_op jit(solution)/shard_map/gather | solution.py:63
  16.4 0.0 copy-done.3
  16.4 24.2 %all-to-all-done = bf16[32,128,128]{2,1,0:T(8,128)(2,1)S(1)} async-done(((bf16[32,128,128]{2,1,0:T(8,128)(2,1)}), bf16[32,128,128]{2,1,0:T(8,128)(2,1)S(1)}, u32[]{:S(2)}, u32[]{:S(2)}) %all-to-all-start) | async-done | bytes 1048608 | tf_op jit(solution)/shard_map/all_to_all | solution.py:16
  40.7 0.6 broadcast_in_dim.15
  41.3 3.9 %all-to-all-start.2 = ((f32[32,1,128]{2,1,0:T(1,128)}), f32[32,1,128]{2,1,0:T(1,128)S(1)}, u32[]{:S(2)}, u32[]{:S(2)}) async-start(f32[32,1,128]{2,1,0:T(1,128)} %broadcast_in_dim.15), calls=%async_computation.2 | async-start | bytes 32768 | tf_op jit(solution)/shard_map/all_to_all | solution.py:16
  45.2 2.7 %gather_fusion = bf16[48,256,128]{2,1,0:T(8,128)(2,1)} fusion(bf16[16,256,128]{2,1,0:T(8,128)(2,1)S(1)} %bitcast.22, s32[1024]{0:T(1024)S(1)} %pad_clamp_fusion.1), kind=kCustom, calls=%fused_computation | custom fusion | bytes 6291648 | tf_op jit(solution)/shard_map/gather | solution.py:73
  47.9 11.7 %fusion.10 = f32[48,256,128]{2,1,0:T(8,128)} fusion(bf16[48,256,128]{2,1,0:T(8,128)(2,1)} %gather_fusion.1, bf16[48,256,256]{2,1,0:T(8,128)(2,1)} %param.6, f32[48]{0:T(128)S(1)} %compare_convert_fusion, bf16[48,256,128]{2,1,0:T(8,128)(2,1)} %gather_fusion), kind=kOutput, calls=%fused_computation.14 | convolution fusion | flops 1623195648 | bytes 18874560 | tf_op jit(solution)/shard_map/nij,njr->nir/dot_general | solution.py:75
  59.6 8.4 %fusion.6 = f32[16,256,128]{2,0,1:T(8,128)S(1)} fusion(f32[48,256,128]{2,1,0:T(8,128)} %fusion.10, s32[48]{0:T(128)S(1)} %copy-done.3), kind=kOutput, calls=%fused_computation.11 | convolution fusion | flops 301990656 | bytes 8388800 | tf_op jit(solution)/shard_map/bn,nir->bir/dot_general | solution.py:76
  67.9 2.0 copy.16
  69.9 0.0 all-to-all-done.2
  69.9 0.0 copy-start.1
  69.9 7.9 %all-to-all-start.1 = ((f32[32,128,128]{2,1,0:T(8,128)}), f32[32,128,128]{2,1,0:T(8,128)S(1)}, u32[]{:S(2)}, u32[]{:S(2)}) async-start(f32[32,128,128]{2,1,0:T(8,128)} %bitcast.4), calls=%async_computation.1 | async-start | bytes 4194304 | tf_op jit(solution)/shard_map/all_to_all | solution.py:43
  77.8 49.7 %all-to-all-done.1 = f32[32,128,128]{2,1,0:T(8,128)S(1)} async-done(((f32[32,128,128]{2,1,0:T(8,128)}), f32[32,128,128]{2,1,0:T(8,128)S(1)}, u32[]{:S(2)}, u32[]{:S(2)}) %all-to-all-start.1) | async-done | bytes 2097184 | tf_op jit(solution)/shard_map/all_to_all | solution.py:43
  127.6 0.1 reduce_sum.45
  127.7 0.0 copy-done.1
  127.7 0.0 copy-start.2
  127.7 0.2 broadcast_in_dim.16
  128.0 32.2 %all_to_all.31 = bf16[32,128,128]{2,1,0:T(8,128)(2,1)S(1)} all-to-all(bf16[32,128,128]{2,1,0:T(8,128)(2,1)S(1)} %broadcast_in_dim.16), channel_id=1, replica_groups=mesh['cell_0'=4,'cell_1'=2,'gene_0'=4,'gene_1'=4,'gene_2'=2] {'gene_0','..., dimensions={0} | all-to-all | bytes 2097152 | tf_op jit(solution)/shard_map/all_to_all | solution.py:16
  160.2 2.7 %gather_fusion.2 = bf16[48,256,128]{2,1,0:T(8,128)(2,1)} fusion(bf16[16,256,128]{2,1,0:T(8,128)(2,1)S(1)} %bitcast.23, s32[1024]{0:T(1024)S(1)} %pad_clamp_fusion.1), kind=kCustom, calls=%fused_computation.2 | custom fusion | bytes 6291648 | tf_op jit(solution)/shard_map/gather | solution.py:83
  162.8 0.0 copy-done.2
  162.8 12.2 %fusion.8 = f32[48,256,128]{2,1,0:T(8,128)} fusion(bf16[48,256,128]{2,1,0:T(8,128)(2,1)} %gather_fusion.2, bf16[48,256,256]{2,1,0:T(8,128)(2,1)} %param.6, f32[48]{0:T(128)S(1)} %compare_convert_fusion, bf16[48,256,128]{2,1,0:T(8,128)(2,1)} %gather_fusion.1), kind=kOutput, calls=%fused_computation.13 | convolution fusion | flops 1623195648 | bytes 18874560 | tf_op jit(solution)/shard_map/nij,nir->njr/dot_general | solution.py:85
  175.1 8.1 %fusion.4 = f32[4,256,128]{2,0,1:T(4,128)S(1)} fusion(f32[48,256,128]{2,1,0:T(8,128)} %fusion.8, s32[48]{0:T(128)S(1)} %copy-done.4), kind=kOutput, calls=%fused_computation.9 | convolution fusion | flops 75497664 | bytes 6815936 | tf_op jit(solution)/shard_map/bn,njr->bjr/dot_general | solution.py:88
  183.2 0.8 copy.20
  184.0 8.1 %all-to-all-start.4 = ((f32[8,128,128]{2,1,0:T(8,128)}), f32[8,128,128]{2,1,0:T(8,128)S(1)}, u32[]{:S(2)}, u32[]{:S(2)}) async-start(f32[8,128,128]{2,1,0:T(8,128)} %bitcast.8), calls=%async_computation.4 | async-start | bytes 1048576 | tf_op jit(solution)/shard_map/all_to_all | solution.py:43
  192.1 9.5 %psum.35 = f32[128]{0:T(128)S(1)} all-reduce(f32[128]{0:T(128)S(1)} %get-tuple-element.2), channel_id=1, replica_groups=mesh['cell_0'=4,'cell_1'=2,'gene_0'=4,'gene_1'=4,'gene_2'=2] {'cell_0'}, use_global_device_ids=true, to_apply=%region_5.0 | all-reduce | flops 128 | bytes 1024 | tf_op jit(solution)/shard_map/psum | solution.py:48
  201.6 7.8 %psum.36 = f32[128]{0:T(128)S(1)} all-reduce(f32[128]{0:T(128)S(1)} %psum.35), channel_id=1, replica_groups=mesh['cell_0'=4,'cell_1'=2,'gene_0'=4,'gene_1'=4,'gene_2'=2] {'cell_1'}, use_global_device_ids=true, to_apply=%region_6.0 | all-reduce | flops 128 | bytes 1024 | tf_op jit(solution)/shard_map/psum | solution.py:48
  209.4 6.7 %psum.37 = f32[128]{0:T(128)S(1)} all-reduce(f32[128]{0:T(128)S(1)} %psum.36), channel_id=1, replica_groups=mesh['cell_0'=4,'cell_1'=2,'gene_0'=4,'gene_1'=4,'gene_2'=2] {'gene_0'}, use_global_device_ids=true, to_apply=%region_7.0 | all-reduce | flops 128 | bytes 1024 | tf_op jit(solution)/shard_map/psum | solution.py:48
  216.1 7.5 %psum.38 = f32[128]{0:T(128)S(1)} all-reduce(f32[128]{0:T(128)S(1)} %psum.37), channel_id=1, replica_groups=mesh['cell_0'=4,'cell_1'=2,'gene_0'=4,'gene_1'=4,'gene_2'=2] {'gene_1'}, use_global_device_ids=true, to_apply=%region_8.0 | all-reduce | flops 128 | bytes 1024 | tf_op jit(solution)/shard_map/psum | solution.py:48
  223.6 9.5 %psum.39 = f32[128]{0:T(128)S(1)} all-reduce(f32[128]{0:T(128)S(1)} %psum.38), channel_id=1, replica_groups=mesh['cell_0'=4,'cell_1'=2,'gene_0'=4,'gene_1'=4,'gene_2'=2] {'gene_2'}, use_global_device_ids=true, to_apply=%region_9.0 | all-reduce | flops 128 | bytes 1024 | tf_op jit(solution)/shard_map/psum | solution.py:48
  233.1 0.0 all-to-all-done.4
  233.2 23.3 %all_to_all.32 = f32[8,128,128]{2,1,0:T(8,128)S(1)} all-to-all(f32[8,128,128]{2,1,0:T(8,128)S(1)} %broadcast_in_dim.17), channel_id=1, replica_groups=mesh['cell_0'=4,'cell_1'=2,'gene_0'=4,'gene_1'=4,'gene_2'=2] {'cell_0','..., dimensions={0} | all-to-all | bytes 1048576 | tf_op jit(solution)/shard_map/all_to_all | solution.py:16
  256.5 0.8 copy.28
  (11 shorter events, 0.2 us)
Async XLA Ops:
  0.6 12.8 %copy-start.4 = (s32[48]{0:T(128)S(1)}, s32[48]{0:T(128)}, u32[]{:S(2)}) copy-start(s32[48]{0:T(128)} %param.8) | copy-start | bytes 580
  0.6 12.9 %copy-start = (f32[1024,128]{1,0:T(8,128)S(1)}, f32[1024,128]{1,0:T(8,128)}, u32[]{:S(2)}) copy-start(f32[1024,128]{1,0:T(8,128)} %param.11) | copy-start | bytes 1572868
  2.8 37.9 %all-to-all-start = ((bf16[32,128,128]{2,1,0:T(8,128)(2,1)}), bf16[32,128,128]{2,1,0:T(8,128)(2,1)S(1)}, u32[]{:S(2)}, u32[]{:S(2)}) async-start(bf16[32,128,128]{2,1,0:T(8,128)(2,1)} %broadcast_in_dim.12), calls=%async_computation | async-start | bytes 2097152 | tf_op jit(solution)/shard_map/all_to_all | solution.py:16
  13.7 2.8 %copy-start.3 = (s32[48]{0:T(128)S(1)}, s32[48]{0:T(128)}, u32[]{:S(2)}) copy-start(s32[48]{0:T(128)} %param.7) | copy-start | bytes 580
  41.3 28.6 %all-to-all-start.2 = ((f32[32,1,128]{2,1,0:T(1,128)}), f32[32,1,128]{2,1,0:T(1,128)S(1)}, u32[]{:S(2)}, u32[]{:S(2)}) async-start(f32[32,1,128]{2,1,0:T(1,128)} %broadcast_in_dim.15), calls=%async_computation.2 | async-start | bytes 32768 | tf_op jit(solution)/shard_map/all_to_all | solution.py:16
  69.9 57.7 %copy-start.1 = (f32[128,128]{1,0:T(8,128)S(1)}, f32[128,128]{1,0:T(8,128)}, u32[]{:S(2)}) copy-start(f32[128,128]{1,0:T(8,128)} %param.10) | copy-start | bytes 196612
  69.9 57.6 %all-to-all-start.1 = ((f32[32,128,128]{2,1,0:T(8,128)}), f32[32,128,128]{2,1,0:T(8,128)S(1)}, u32[]{:S(2)}, u32[]{:S(2)}) async-start(f32[32,128,128]{2,1,0:T(8,128)} %bitcast.4), calls=%async_computation.1 | async-start | bytes 4194304 | tf_op jit(solution)/shard_map/all_to_all | solution.py:43
  127.7 35.1 %copy-start.2 = (f32[128,128]{1,0:T(8,128)}, f32[128,128]{1,0:T(8,128)S(1)}, u32[]{:S(2)}) copy-start(f32[128,128]{1,0:T(8,128)S(1)} %get-tuple-element.8) | copy-start | bytes 196612
  184.0 49.1 %all-to-all-start.4 = ((f32[8,128,128]{2,1,0:T(8,128)}), f32[8,128,128]{2,1,0:T(8,128)S(1)}, u32[]{:S(2)}, u32[]{:S(2)}) async-start(f32[8,128,128]{2,1,0:T(8,128)} %bitcast.8), calls=%async_computation.4 | async-start | bytes 1048576 | tf_op jit(solution)/shard_map/all_to_all | solution.py:43
where the time goes:
time: 259 us; the launch traced here: 257 us
  blocking collectives  96.4 us (37%)
  waiting for transfers between devices  74 us (29%)
  matrix products  40.4 us (16%)
  starting transfers between devices  29.9 us (12%)
  local copies, waits for them, and re-layouts  13.8 us (5%)
    all_to_all x2, blocking collectives, sent_to_all(): lax.all_to_all(jnp.broadcast_to(shard[None], (count, *shard.shape)), axis...  55.4 us
    all_to_all x2, waiting for transfers between devices, sent_and_summed(): lax.all_to_all(blocks, axis, split_axis=0, concat_axis=0, tiled=True)  49.7 us
    psum x5, blocking collectives, by_axis(): return functools.reduce(lax.psum, axes, shard)  40.9 us
    all_to_all x2, waiting for transfers between devices, sent_to_all(): lax.all_to_all(jnp.broadcast_to(shard[None], (count, *shard.shape)), axis...  24.2 us
    all_to_all x2, starting transfers between devices, sent_and_summed(): lax.all_to_all(blocks, axis, split_axis=0, concat_axis=0, tiled=True)  16 us
    all_to_all x2, starting transfers between devices, sent_to_all(): lax.all_to_all(jnp.broadcast_to(shard[None], (count, *shard.shape)), axis...  13.9 us
    dot_general x1, matrix products, on_device(): jnp.einsum('nij,nir->njr', ratio_next, new_tiles, preferred_element_type=...  12.2 us
    dot_general x1, matrix products, on_device(): jnp.einsum('nij,njr->nir', ratio, gene_tiles, preferred_element_type=jnp....  11.7 us
  transfers between devices with their start and end apart: 4, of which 2 were waited for; matrix products, arithmetic and copies ran while one was open for 11% of the time, Pallas kernels for 0%

commit v1 on v0

v1 whole, which is shorter than its diff:
```python
import jax
import jax.numpy as jnp
from jax import lax
from jax.experimental import pallas as pl
from jax.experimental.pallas import tpu as pltpu
from jax.sharding import Mesh
from jax.sharding import PartitionSpec as P

GENE = ("x", "zl", "c")
CELL_GENE = ("y", "zh", "x", "zl", "c")

BLK = 256
R = 128
NB = 48
HALF = 128
PAD = 144
UNITS = 32
PAIR = 2
BF = jnp.bfloat16
F32 = jnp.float32
NT = (((1,), (1,)), ((), ()))
VMEM_LIMIT = 48 * 1024 * 1024


def shift(value, axis, step):
    count = lax.axis_size(axis)
    return lax.ppermute(value, axis, [(i, (i + step) % count) for i in range(count)])


def gathered(payload):
    for axis in ("zl", "x", "c"):
        parts = [payload] + [shift(payload, axis, k) for k in range(1, lax.axis_size(axis))]
        payload = jnp.concatenate(parts, 0)
    return payload


def three_pieces(total):
    hi = total.astype(BF)
    rest = total - hi.astype(F32)
    mid = rest.astype(BF)
    lo = (rest - mid.astype(F32)).astype(BF)
    wide = lambda a: jnp.concatenate([a.astype(F32)] * 2, 0)
    which = lax.broadcasted_iota(jnp.int32, (16, R), 0)
    rows = jnp.where(
        which == 0,
        wide(hi),
        jnp.where(which == 1, wide(mid), jnp.where(which == 2, wide(lo), 0.0)),
    )
    return rows.astype(BF)


def column_sum(value):
    return jnp.broadcast_to(jnp.sum(value, 0, keepdims=True), (8, R))


def joined(pieces):
    return column_sum(pieces.astype(F32))


def prep_kernel(cell_ref, gene_ref, pay_ref):
    pay_ref[:HALF, :] = cell_ref[...].astype(BF)
    pay_ref[HALF:, :] = three_pieces(column_sum(gene_ref[...]))


def slot_base(meta, row, parity):
    dx = (meta[0] - (row >> 2)) & 3
    dz = (meta[1] - (row & 3)) & 3
    dc = meta[2] ^ parity
    return pl.multiple_of((dc * 16 + dx * 4 + dz) * PAD, 16)


def unit_base(meta, row, parity):
    dx = ((row >> 2) - meta[0]) & 3
    dz = ((row & 3) - meta[1]) & 3
    dc = meta[2] ^ parity
    return pl.multiple_of((dc * 16 + dx * 4 + dz) * HALF, HALF)


def fetch_all(blocks_ref, tiles, sems):
    def start(s, carry):
        pltpu.make_async_copy(blocks_ref.at[s], tiles.at[s], sems.at[s]).start()
        return carry

    lax.fori_loop(0, NB, start, 0)


def await_tile(blocks_ref, tiles, sems, s):
    pltpu.make_async_copy(blocks_ref.at[s], tiles.at[s], sems.at[s]).wait()


def ratio_of(tile, w, h, live):
    model = lax.dot_general(w, h, NT, preferred_element_type=F32)
    return (tile.astype(F32) / model * live).astype(BF)


def group_sum(g_ref):
    def add(u, total):
        return total + g_ref[pl.ds(pl.multiple_of(u * PAD + HALF, 16), 16), :].astype(F32)

    total = lax.fori_loop(0, UNITS, add, jnp.zeros((16, R), F32))
    return column_sum(total)


def over_slots(count, meta, blocks_ref, tiles, sems, body):
    steps = (count + PAIR - 1) // PAIR

    def step(p, carry):
        for k in range(PAIR):
            await_tile(blocks_ref, tiles, sems, p * PAIR + k)
        for k in range(PAIR):
            body(p * PAIR + k)
        return carry

    lax.fori_loop(0, steps, step, 0)

    def drain(s, carry):
        await_tile(blocks_ref, tiles, sems, s)
        return carry

    lax.fori_loop(steps * PAIR, NB, drain, 0)


def cells_kernel(
    meta, rows, cols, blocks_ref, g_ref, gene_ref, keep_ref, send_ref, sum_ref, tiles, hb, acc, sems
):
    fetch_all(blocks_ref, tiles, sems)
    hb[...] = gene_ref[...].astype(BF)
    acc[...] = jnp.zeros_like(acc)
    sum_ref[...] = group_sum(g_ref)
    count = meta[3]

    def body(s):
        row = rows[s]
        live = jnp.where(s < count, 1.0, 0.0).astype(F32)
        h = hb[pl.ds(pl.multiple_of(cols[s] * BLK, BLK), BLK), :]
        w = jnp.concatenate(
            [g_ref[pl.ds(slot_base(meta, row, parity), HALF), :] for parity in (0, 1)], 0
        )
        ratio = ratio_of(tiles[s], w, h, live)
        terms = jnp.dot(ratio, h, preferred_element_type=F32)
        for parity in (0, 1):
            at = pl.ds(unit_base(meta, row, parity), HALF)
            acc[at, :] = acc[at, :] + terms[parity * HALF : (parity + 1) * HALF]

    over_slots(count, meta, blocks_ref, tiles, sems, body)
    half = UNITS // 2 * HALF
    keep_ref[...] = acc[:half, :]
    send_ref[...] = acc[half:, :].astype(BF)


def update_kernel(own_ref, r1_ref, r2_ref, r3_ref, cell_ref, sum_ref, new_ref, pay_ref):
    numer = own_ref[...] + r1_ref[...] + r2_ref[...] + r3_ref[...]
    new = cell_ref[...] * numer / sum_ref[0:1, :]
    new_ref[...] = new
    pay_ref[:HALF, :] = new.astype(BF)
    pay_ref[HALF:, :] = three_pieces(column_sum(new))


def genes_kernel(
    meta, rows, cols, blocks_ref, g_ref, gene_ref, own_ref, send_ref, sum_ref, tiles, hb, wt, acc, sems
):
    fetch_all(blocks_ref, tiles, sems)
    hb[...] = gene_ref[...].astype(BF)
    acc[...] = jnp.zeros_like(acc)
    total = group_sum(g_ref)
    sum_ref[...] = total
    count = meta[3]

    def load_w(row):
        return jnp.concatenate(
            [g_ref[pl.ds(slot_base(meta, row, parity), HALF), :] for parity in (0, 1)], 0
        )

    def turn(row, carry):
        wt[row] = load_w(row).T
        return carry

    lax.fori_loop(0, wt.shape[0], turn, 0)

    def body(s):
        row = rows[s]
        live = jnp.where(s < count, 1.0, 0.0).astype(F32)
        h = hb[pl.ds(pl.multiple_of(cols[s] * BLK, BLK), BLK), :]
        ratio = ratio_of(tiles[s], load_w(row), h, live)
        at = (cols[s] - meta[4]) & 3
        acc[at] = acc[at] + jnp.dot(wt[row], ratio, preferred_element_type=F32)

    over_slots(count, meta, blocks_ref, tiles, sems, body)
    own_ref[...] = acc[0].T
    pieces = three_pieces(total)
    for k in range(1, 4):
        send_ref[k - 1, :BLK, :] = acc[k].T.astype(BF)
        send_ref[k - 1, BLK:, :] = pieces


def fold_kernel(own_ref, sum_ref, r1_ref, r2_ref, r3_ref, out_ref):
    numer = own_ref[...]
    total = sum_ref[...]
    for ref in (r1_ref, r2_ref, r3_ref):
        numer = numer + ref[:BLK, :].astype(F32)
        total = total + joined(ref[BLK:, :])
    out_ref[:BLK, :] = numer
    out_ref[BLK:, :] = total


def finish_kernel(meta, mine_ref, other_ref, gene_ref, out_ref):
    both = mine_ref[...] + other_ref[...]
    at = pl.ds(pl.multiple_of(meta[4] * BLK, BLK), BLK)
    out_ref[...] = gene_ref[at, :] * both[:BLK] / both[BLK : BLK + 1]


def place_kernel(meta, p0_ref, p1_ref, p2_ref, p3_ref, out_ref):
    for k, ref in enumerate((p0_ref, p1_ref, p2_ref, p3_ref)):
        at = pl.ds(pl.multiple_of(((meta[4] - k) & 3) * BLK, BLK), BLK)
        out_ref[at, :] = ref[...]


def vspec():
    return pl.BlockSpec(memory_space=pltpu.VMEM)


def sspec():
    return pl.BlockSpec(memory_space=pltpu.SMEM)


def call(kernel, outs, args, kinds, scratch=(), name=None):
    spec = {"s": sspec, "v": vspec, "a": lambda: pl.BlockSpec(memory_space=pl.ANY)}
    return pl.pallas_call(
        kernel,
        out_shape=outs,
        in_specs=[spec[kind]() for kind in kinds],
        out_specs=jax.tree.map(lambda _: vspec(), outs),
        scratch_shapes=list(scratch),
        name=name,
        compiler_params=pltpu.CompilerParams(vmem_limit_bytes=VMEM_LIMIT),
    )(*args)


def shape(dims, dtype):
    return jax.ShapeDtypeStruct(dims, dtype)


def on_device(blocks, block_rows, block_cols, block_count, cell_factor, gene_factor):
    genes = gene_factor.shape[0]
    half = UNITS // 2 * HALF
    meta = jnp.stack(
        [
            lax.axis_index("x"),
            lax.axis_index("zl"),
            lax.axis_index("c"),
            block_count[0],
            lax.axis_index("y"),
        ]
    ).astype(jnp.int32)
    pay = call(prep_kernel, shape((PAD, R), BF), (cell_factor, gene_factor), "vv", name="prep")
    g1 = gathered(pay)
    common = [pltpu.VMEM((NB, BLK, BLK), BF), pltpu.VMEM((genes, R), BF)]
    keep, send, gene_sums = call(
        cells_kernel,
        (shape((half, R), F32), shape((half, R), BF), shape((8, R), F32)),
        (meta, block_rows, block_cols, blocks, g1, gene_factor),
        "sssavv",
        common + [pltpu.VMEM((2 * half, R), F32), pltpu.SemaphoreType.DMA((NB,))],
        name="cells",
    )
    part = keep + shift(send, "c", 1).astype(F32)
    quarter = half // 4
    sent = [shift(part[k * quarter : (k + 1) * quarter].astype(BF), "x", k) for k in (1, 2, 3)]
    part = part[:quarter]
    for arrived in sent:
        part = part + arrived.astype(F32)
    own = part[:HALF]
    sent = [shift(part[k * HALF : (k + 1) * HALF], "zl", k) for k in (1, 2, 3)]
    cell_new, pay = call(
        update_kernel,
        (shape((HALF, R), F32), shape((PAD, R), BF)),
        (own, *sent, cell_factor, gene_sums),
        "vvvvvv",
        name="update",
    )
    g2 = gathered(pay)
    mine, send, cell_part = call(
        genes_kernel,
        (shape((BLK, R), F32), shape((3, BLK + 16, R), BF), shape((8, R), F32)),
        (meta, block_rows, block_cols, blocks, g2, gene_factor),
        "sssavv",
        common
        + [
            pltpu.VMEM((16, R, BLK), BF),
            pltpu.VMEM((4, R, BLK), F32),
            pltpu.SemaphoreType.DMA((NB,)),
        ],
        name="genes",
    )
    arrived = [shift(send[k - 1], "y", k) for k in (1, 2, 3)]
    folded = call(
        fold_kernel, shape((BLK + 8, R), F32), (mine, cell_part, *arrived), "vvvvv", name="fold"
    )
    other = shift(folded, "zh", 1)
    fresh = call(
        finish_kernel,
        shape((BLK, R), F32),
        (meta, folded, other, gene_factor),
        "svvv",
        name="finish",
    )
    parts = [fresh] + [shift(fresh, "y", k) for k in (1, 2, 3)]
    gene_new = call(
        place_kernel, shape((genes, R), F32), (meta, *parts), "svvvv", name="place"
    )
    return (cell_new, gene_new)


def solution(mesh):
    torus = Mesh(mesh.devices.reshape(4, 2, 4, 4, 2), CELL_GENE)
    return jax.shard_map(
        on_device,
        mesh=torus,
        in_specs=(
            P(CELL_GENE, None, None),
            P(CELL_GENE),
            P(CELL_GENE),
            P(CELL_GENE),
            P(CELL_GENE, None),
            P(GENE, None),
        ),
        out_specs=(P(CELL_GENE, None), P(GENE, None)),
        check_vma=False,
    )
```

time: 259 us -> 122 us (0.47)
  the two profiles are of different devices: /device:TPU:1 before, /device:TPU:6 now
where the time goes in v1:
time: 122 us; the launch traced here: 124 us
  waiting for transfers between devices  55.1 us (45%)
  starting transfers between devices  36.6 us (30%)
  Pallas kernels  27.6 us (23%)
  local copies, waits for them, and re-layouts  2.58 us (2%)
  between operations  1.51 us (1%)
    ppermute x28, waiting for transfers between devices, shift(): lax.ppermute(value, axis, [(i, (i + step) % count) for i in range(count)])  55.1 us
    ppermute x28, starting transfers between devices, shift(): lax.ppermute(value, axis, [(i, (i + step) % count) for i in range(count)])  36.6 us
    pallas_call x7, Pallas kernels, call(): pl.pallas_call(kernel, out_shape=outs, in_specs=[spec[kind]() for kind in...  27.6 us
  transfers between devices with their start and end apart: 28, of which 25 were waited for; matrix products, arithmetic and copies ran while one was open for 0% of the time, Pallas kernels for 0%

profile of v1, /device:TPU:6, one launch (start us, length us, event | category | flops | bytes accessed | tf_op | source)
XLA Modules:
  0.0 123.5 jit_solution(16040967333603105012)
XLA Ops:
  0.6 1.0 copy-done
  1.7 0.8 copy-done.2
  2.7 2.0 %collective-permute-start = (bf16[144,128]{1,0:T(8,128)(2,1)S(1)}, bf16[144,128]{1,0:T(8,128)(2,1)S(1)}, u32[]{:S(2)}, u32[]{:S(2)}) collective-permute-start(bf16[144,128]{1,0:T(8,128)(2,1)S(1)} %prep.1), channel_id=1, source_target_pairs={{0,2},{2,4},{4,6},{6,0},{1,3},{3,5},{5,7},{7,1},{8,10},{10,12},{12... | collective-permute-start | bytes 110600 | tf_op jit(solution)/shard_map/ppermute | solution.py:27
  4.7 3.3 %collective-permute-start.1 = (bf16[144,128]{1,0:T(8,128)(2,1)S(1)}, bf16[144,128]{1,0:T(8,128)(2,1)S(1)}, u32[]{:S(2)}, u32[]{:S(2)}) collective-permute-start(bf16[144,128]{1,0:T(8,128)(2,1)S(1)} %prep.1), channel_id=1, source_target_pairs={{0,4},{2,6},{4,0},{6,2},{1,5},{3,7},{5,1},{7,3},{8,12},{10,14},{12... | collective-permute-start | bytes 110600 | tf_op jit(solution)/shard_map/ppermute | solution.py:27
  7.9 1.0 collective-permute-start.2
  8.9 0.6 collective-permute-done
  9.5 0.9 collective-permute-done.1
  10.5 1.4 %collective-permute-done.2 = bf16[144,128]{1,0:T(8,128)(2,1)S(1)} collective-permute-done((bf16[144,128]{1,0:T(8,128)(2,1)S(1)}, bf16[144,128]{1,0:T(8,128)(2,1)S(1)}, u32[]{:S(2)}, u32[]{:S(2)}) %collective-permute-start.2) | collective-permute-done | bytes 36896 | tf_op jit(solution)/shard_map/ppermute | solution.py:27
  12.5 2.4 %collective-permute-start.4 = (bf16[576,128]{1,0:T(8,128)(2,1)S(1)}, bf16[576,128]{1,0:T(8,128)(2,1)S(1)}, u32[]{:S(2)}, u32[]{:S(2)}) collective-permute-start(bf16[576,128]{1,0:T(8,128)(2,1)S(1)} %pad_maximum_fusion), channel_id=1, source_target_pairs={{0,16},{8,24},{16,0},{24,8},{1,17},{9,25},{17,1},{25,9},{2,18},{10... | collective-permute-start | bytes 442376 | tf_op jit(solution)/shard_map/ppermute | solution.py:27
  14.9 3.1 %collective-permute-done.3 = bf16[576,128]{1,0:T(8,128)(2,1)S(1)} collective-permute-done((bf16[576,128]{1,0:T(8,128)(2,1)S(1)}, bf16[576,128]{1,0:T(8,128)(2,1)S(1)}, u32[]{:S(2)}, u32[]{:S(2)}) %collective-permute-start.3) | collective-permute-done | bytes 147488 | tf_op jit(solution)/shard_map/ppermute | solution.py:27
  18.1 2.0 %collective-permute-done.4 = bf16[576,128]{1,0:T(8,128)(2,1)S(1)} collective-permute-done((bf16[576,128]{1,0:T(8,128)(2,1)S(1)}, bf16[576,128]{1,0:T(8,128)(2,1)S(1)}, u32[]{:S(2)}, u32[]{:S(2)}) %collective-permute-start.4) | collective-permute-done | bytes 147488 | tf_op jit(solution)/shard_map/ppermute | solution.py:27
  20.1 1.5 %collective-permute-done.5 = bf16[576,128]{1,0:T(8,128)(2,1)S(1)} collective-permute-done((bf16[576,128]{1,0:T(8,128)(2,1)S(1)}, bf16[576,128]{1,0:T(8,128)(2,1)S(1)}, u32[]{:S(2)}, u32[]{:S(2)}) %collective-permute-start.5) | collective-permute-done | bytes 147488 | tf_op jit(solution)/shard_map/ppermute | solution.py:27
  22.5 1.3 %collective-permute-done.6 = bf16[2304,128]{1,0:T(8,128)(2,1)S(1)} collective-permute-done((bf16[2304,128]{1,0:T(8,128)(2,1)S(1)}, bf16[2304,128]{1,0:T(8,128)(2,1)S(1)}, u32[]{:S(2)}, u32[]{:S(2)}) %collective-permute-start.6) | collective-permute-done | bytes 589856 | tf_op jit(solution)/shard_map/ppermute | solution.py:27
  23.8 11.4 %cells.1 = (f32[2048,128]{1,0:T(8,128)S(1)}, bf16[2048,128]{1,0:T(8,128)(2,1)S(1)}, f32[8,128]{1,0:T(8,128)S(1)}) custom-call(s32[5]{0:T(128)S(1)} %stack.19.meta, s32[48]{0:T(128)S(1)} %copy-done.4, s32[48]{0:T(128)S(1)} %copy-done.5, bf16[48,256,256]{2,1,0:T(8,128)(2,1)} %blocks_ref.3, bf16[4608,128]{1,0:T(8,128)(2,1)S(1)} %constant_dynamic-update-slice_fusion.7.g_ref, ...), custom_call_target="tpu_custom_call" | custom-call | tf_op jit(solution)/shard_map/cells/pallas_call | solution.py:228
  35.3 1.9 %collective-permute-done.7 = bf16[2048,128]{1,0:T(8,128)(2,1)S(1)} collective-permute-done((bf16[2048,128]{1,0:T(8,128)(2,1)S(1)}, bf16[2048,128]{1,0:T(8,128)(2,1)S(1)}, u32[]{:S(2)}, u32[]{:S(2)}) %collective-permute-start.7) | collective-permute-done | bytes 524320 | tf_op jit(solution)/shard_map/ppermute | solution.py:27
  37.5 1.1 collective-permute-start.9
  38.6 2.1 %collective-permute-start.8 = (bf16[512,128]{1,0:T(8,128)(2,1)S(1)}, bf16[512,128]{1,0:T(8,128)(2,1)S(1)}, u32[]{:S(2)}, u32[]{:S(2)}) collective-permute-start(bf16[512,128]{1,0:T(8,128)(2,1)S(1)} %get-tuple-element.20), channel_id=1, source_target_pairs={{0,8},{8,16},{16,24},{24,0},{1,9},{9,17},{17,25},{25,1},{2,10},{10... | collective-permute-start | bytes 393224 | tf_op jit(solution)/shard_map/ppermute | solution.py:27
  40.7 6.3 %collective-permute-done.10 = bf16[512,128]{1,0:T(8,128)(2,1)S(1)} collective-permute-done((bf16[512,128]{1,0:T(8,128)(2,1)S(1)}, bf16[512,128]{1,0:T(8,128)(2,1)S(1)}, u32[]{:S(2)}, u32[]{:S(2)}) %collective-permute-start.10) | collective-permute-done | bytes 131104 | tf_op jit(solution)/shard_map/ppermute | solution.py:27
  47.1 0.6 collective-permute-done.8
  47.8 1.8 %collective-permute-start.11 = (f32[128,128]{1,0:T(8,128)S(1)}, f32[128,128]{1,0:T(8,128)S(1)}, u32[]{:S(2)}, u32[]{:S(2)}) collective-permute-start(f32[128,128]{1,0:T(8,128)S(1)} %get-tuple-element.25), channel_id=1, source_target_pairs={{0,2},{2,4},{4,6},{6,0},{1,3},{3,5},{5,7},{7,1},{8,10},{10,12},{12... | collective-permute-start | bytes 196616 | tf_op jit(solution)/shard_map/ppermute | solution.py:27
  49.6 2.5 %collective-permute-start.13 = (f32[128,128]{1,0:T(8,128)S(1)}, f32[128,128]{1,0:T(8,128)S(1)}, u32[]{:S(2)}, u32[]{:S(2)}) collective-permute-start(f32[128,128]{1,0:T(8,128)S(1)} %get-tuple-element.23), channel_id=1, source_target_pairs={{0,6},{2,0},{4,2},{6,4},{1,7},{3,1},{5,3},{7,5},{8,14},{10,8},{12,... | collective-permute-start | bytes 196616 | tf_op jit(solution)/shard_map/ppermute | solution.py:27
  52.0 2.6 %collective-permute-done.11.r1_ref = f32[128,128]{1,0:T(8,128)S(1)} collective-permute-done((f32[128,128]{1,0:T(8,128)S(1)}, f32[128,128]{1,0:T(8,128)S(1)}, u32[]{:S(2)}, u32[]{:S(2)}) %collective-permute-start.11) | collective-permute-done | bytes 65568 | tf_op jit(solution)/shard_map/ppermute | solution.py:27
  54.6 1.6 %collective-permute-done.12.r2_ref = f32[128,128]{1,0:T(8,128)S(1)} collective-permute-done((f32[128,128]{1,0:T(8,128)S(1)}, f32[128,128]{1,0:T(8,128)S(1)}, u32[]{:S(2)}, u32[]{:S(2)}) %collective-permute-start.12) | collective-permute-done | bytes 65568 | tf_op jit(solution)/shard_map/ppermute | solution.py:27
  56.2 0.7 update.1
  56.8 1.3 %collective-permute-start.14 = (bf16[144,128]{1,0:T(8,128)(2,1)S(1)}, bf16[144,128]{1,0:T(8,128)(2,1)S(1)}, u32[]{:S(2)}, u32[]{:S(2)}) collective-permute-start(bf16[144,128]{1,0:T(8,128)(2,1)S(1)} %get-tuple-element.14), channel_id=1, source_target_pairs={{0,2},{2,4},{4,6},{6,0},{1,3},{3,5},{5,7},{7,1},{8,10},{10,12},{12... | collective-permute-start | bytes 110600 | tf_op jit(solution)/shard_map/ppermute | solution.py:27
  58.1 1.8 %collective-permute-start.15 = (bf16[144,128]{1,0:T(8,128)(2,1)S(1)}, bf16[144,128]{1,0:T(8,128)(2,1)S(1)}, u32[]{:S(2)}, u32[]{:S(2)}) collective-permute-start(bf16[144,128]{1,0:T(8,128)(2,1)S(1)} %get-tuple-element.14), channel_id=1, source_target_pairs={{0,4},{2,6},{4,0},{6,2},{1,5},{3,7},{5,1},{7,3},{8,12},{10,14},{12... | collective-permute-start | bytes 110600 | tf_op jit(solution)/shard_map/ppermute | solution.py:27
  60.0 1.1 collective-permute-start.16
  61.0 1.6 %collective-permute-done.14 = bf16[144,128]{1,0:T(8,128)(2,1)S(1)} collective-permute-done((bf16[144,128]{1,0:T(8,128)(2,1)S(1)}, bf16[144,128]{1,0:T(8,128)(2,1)S(1)}, u32[]{:S(2)}, u32[]{:S(2)}) %collective-permute-start.14) | collective-permute-done | bytes 36896 | tf_op jit(solution)/shard_map/ppermute | solution.py:27
  62.6 0.8 collective-permute-done.15
  63.9 2.9 %collective-permute-start.17 = (bf16[576,128]{1,0:T(8,128)(2,1)S(1)}, bf16[576,128]{1,0:T(8,128)(2,1)S(1)}, u32[]{:S(2)}, u32[]{:S(2)}) collective-permute-start(bf16[576,128]{1,0:T(8,128)(2,1)S(1)} %get-tuple-element.44), channel_id=1, source_target_pairs={{0,8},{8,16},{16,24},{24,0},{1,9},{9,17},{17,25},{25,1},{2,10},{10... | collective-permute-start | bytes 442376 | tf_op jit(solution)/shard_map/ppermute | solution.py:27
  66.9 1.0 collective-permute-start.19
  67.8 4.4 %collective-permute-done.17 = bf16[576,128]{1,0:T(8,128)(2,1)S(1)} collective-permute-done((bf16[576,128]{1,0:T(8,128)(2,1)S(1)}, bf16[576,128]{1,0:T(8,128)(2,1)S(1)}, u32[]{:S(2)}, u32[]{:S(2)}) %collective-permute-start.17) | collective-permute-done | bytes 147488 | tf_op jit(solution)/shard_map/ppermute | solution.py:27
  72.3 2.1 %collective-permute-done.18 = bf16[576,128]{1,0:T(8,128)(2,1)S(1)} collective-permute-done((bf16[576,128]{1,0:T(8,128)(2,1)S(1)}, bf16[576,128]{1,0:T(8,128)(2,1)S(1)}, u32[]{:S(2)}, u32[]{:S(2)}) %collective-permute-start.18) | collective-permute-done | bytes 147488 | tf_op jit(solution)/shard_map/ppermute | solution.py:27
  74.5 1.2 collective-permute-done.19
  75.9 2.0 %collective-permute-done.20 = bf16[2304,128]{1,0:T(8,128)(2,1)S(1)} collective-permute-done((bf16[2304,128]{1,0:T(8,128)(2,1)S(1)}, bf16[2304,128]{1,0:T(8,128)(2,1)S(1)}, u32[]{:S(2)}, u32[]{:S(2)}) %collective-permute-start.20) | collective-permute-done | bytes 589856 | tf_op jit(solution)/shard_map/ppermute | solution.py:27
  77.9 13.4 %genes.1 = (f32[256,128]{1,0:T(8,128)S(1)}, bf16[3,272,128]{2,1,0:T(8,128)(2,1)S(1)}, f32[8,128]{1,0:T(8,128)S(1)}) custom-call(s32[5]{0:T(128)S(1)} %stack.19.meta, s32[48]{0:T(128)S(1)} %copy-done.4, s32[48]{0:T(128)S(1)} %copy-done.5, bf16[48,256,256]{2,1,0:T(8,128)(2,1)} %blocks_ref.3, bf16[4608,128]{1,0:T(8,128)(2,1)S(1)} %constant_dynamic-update-slice_fusion.26.g_ref, ...), custom_call_target="tpu_custom_call" | custom-call | tf_op jit(solution)/shard_map/genes/pallas_call | solution.py:228
  91.4 4.4 %collective-permute-start.22 = (bf16[272,128]{1,0:T(8,128)(2,1)S(1)}, bf16[272,128]{1,0:T(8,128)(2,1)S(1)}, u32[]{:S(2)}, u32[]{:S(2)}) collective-permute-start(bf16[272,128]{1,0:T(8,128)(2,1)S(1)} %get-tuple-element.28), channel_id=1, source_target_pairs={{0,128},{64,192},{128,0},{192,64},{1,129},{65,193},{129,1},{193,65... | collective-permute-start | bytes 208904 | tf_op jit(solution)/shard_map/ppermute | solution.py:27
  95.8 1.1 collective-permute-done.21.r1_ref
  96.9 3.3 %collective-permute-done.22.r2_ref = bf16[272,128]{1,0:T(8,128)(2,1)S(1)} collective-permute-done((bf16[272,128]{1,0:T(8,128)(2,1)S(1)}, bf16[272,128]{1,0:T(8,128)(2,1)S(1)}, u32[]{:S(2)}, u32[]{:S(2)}) %collective-permute-start.22) | collective-permute-done | bytes 69664 | tf_op jit(solution)/shard_map/ppermute | solution.py:27
  100.3 2.3 %collective-permute-start.24 = (f32[264,128]{1,0:T(8,128)S(1)}, f32[264,128]{1,0:T(8,128)S(1)}, u32[]{:S(2)}, u32[]{:S(2)}) collective-permute-start(f32[264,128]{1,0:T(8,128)S(1)} %fold.1.mine_ref), channel_id=1, source_target_pairs={{0,32},{32,0},{1,33},{33,1},{2,34},{34,2},{3,35},{35,3},{4,36},{36... | collective-permute-start | bytes 405512 | tf_op jit(solution)/shard_map/ppermute | solution.py:27
  102.6 8.6 %collective-permute-done.24.other_ref = f32[264,128]{1,0:T(8,128)S(1)} collective-permute-done((f32[264,128]{1,0:T(8,128)S(1)}, f32[264,128]{1,0:T(8,128)S(1)}, u32[]{:S(2)}, u32[]{:S(2)}) %collective-permute-start.24) | collective-permute-done | bytes 135200 | tf_op jit(solution)/shard_map/ppermute | solution.py:27
  111.2 0.6 finish.1.p0_ref
  111.8 0.6 collective-permute-start.25
  112.4 3.5 %collective-permute-start.26 = (f32[256,128]{1,0:T(8,128)S(1)}, f32[256,128]{1,0:T(8,128)S(1)}, u32[]{:S(2)}, u32[]{:S(2)}) collective-permute-start(f32[256,128]{1,0:T(8,128)S(1)} %finish.1.p0_ref), channel_id=1, source_target_pairs={{0,128},{64,192},{128,0},{192,64},{1,129},{65,193},{129,1},{193,65... | collective-permute-start | bytes 393224 | tf_op jit(solution)/shard_map/ppermute | solution.py:27
  115.9 0.6 collective-permute-start.27
  116.5 1.7 %collective-permute-done.25.p1_ref = f32[256,128]{1,0:T(8,128)S(1)} collective-permute-done((f32[256,128]{1,0:T(8,128)S(1)}, f32[256,128]{1,0:T(8,128)S(1)}, u32[]{:S(2)}, u32[]{:S(2)}) %collective-permute-start.25) | collective-permute-done | bytes 131104 | tf_op jit(solution)/shard_map/ppermute | solution.py:27
  118.2 4.0 %collective-permute-done.26.p2_ref = f32[256,128]{1,0:T(8,128)S(1)} collective-permute-done((f32[256,128]{1,0:T(8,128)S(1)}, f32[256,128]{1,0:T(8,128)S(1)}, u32[]{:S(2)}, u32[]{:S(2)}) %collective-permute-start.26) | collective-permute-done | bytes 131104 | tf_op jit(solution)/shard_map/ppermute | solution.py:27
  122.2 1.4 %place.1 = f32[1024,128]{1,0:T(8,128)} custom-call(s32[5]{0:T(128)S(1)} %stack.19.meta, f32[256,128]{1,0:T(8,128)S(1)} %finish.1.p0_ref, f32[256,128]{1,0:T(8,128)S(1)} %collective-permute-done.25.p1_ref, f32[256,128]{1,0:T(8,128)S(1)} %collective-permute-done.26.p2_ref, f32[256,128]{1,0:T(8,128)S(1)} %collective-permute-done.27.p3_ref), custom_call_target="tpu_custom_call" | custom-call | tf_op jit(solution)/shard_map/place/pallas_call | solution.py:228
  (50 shorter events, 2.7 us)
Async XLA Ops:
  0.6 1.0 copy-start
  1.7 0.8 copy-start.2
  2.7 6.9 %collective-permute-start = (bf16[144,128]{1,0:T(8,128)(2,1)S(1)}, bf16[144,128]{1,0:T(8,128)(2,1)S(1)}, u32[]{:S(2)}, u32[]{:S(2)}) collective-permute-start(bf16[144,128]{1,0:T(8,128)(2,1)S(1)} %prep.1), channel_id=1, source_target_pairs={{0,2},{2,4},{4,6},{6,0},{1,3},{3,5},{5,7},{7,1},{8,10},{10,12},{12... | collective-permute-start | bytes 110600 | tf_op jit(solution)/shard_map/ppermute | solution.py:27
  4.7 5.8 %collective-permute-start.1 = (bf16[144,128]{1,0:T(8,128)(2,1)S(1)}, bf16[144,128]{1,0:T(8,128)(2,1)S(1)}, u32[]{:S(2)}, u32[]{:S(2)}) collective-permute-start(bf16[144,128]{1,0:T(8,128)(2,1)S(1)} %prep.1), channel_id=1, source_target_pairs={{0,4},{2,6},{4,0},{6,2},{1,5},{3,7},{5,1},{7,3},{8,12},{10,14},{12... | collective-permute-start | bytes 110600 | tf_op jit(solution)/shard_map/ppermute | solution.py:27
  7.9 4.0 %collective-permute-start.2 = (bf16[144,128]{1,0:T(8,128)(2,1)S(1)}, bf16[144,128]{1,0:T(8,128)(2,1)S(1)}, u32[]{:S(2)}, u32[]{:S(2)}) collective-permute-start(bf16[144,128]{1,0:T(8,128)(2,1)S(1)} %prep.1), channel_id=1, source_target_pairs={{0,6},{2,0},{4,2},{6,4},{1,7},{3,1},{5,3},{7,5},{8,14},{10,8},{12,... | collective-permute-start | bytes 110600 | tf_op jit(solution)/shard_map/ppermute | solution.py:27
  11.9 6.1 %collective-permute-start.3 = (bf16[576,128]{1,0:T(8,128)(2,1)S(1)}, bf16[576,128]{1,0:T(8,128)(2,1)S(1)}, u32[]{:S(2)}, u32[]{:S(2)}) collective-permute-start(bf16[576,128]{1,0:T(8,128)(2,1)S(1)} %pad_maximum_fusion), channel_id=1, source_target_pairs={{0,8},{8,16},{16,24},{24,0},{1,9},{9,17},{17,25},{25,1},{2,10},{10... | collective-permute-start | bytes 442376 | tf_op jit(solution)/shard_map/ppermute | solution.py:27
  12.5 7.6 %collective-permute-start.4 = (bf16[576,128]{1,0:T(8,128)(2,1)S(1)}, bf16[576,128]{1,0:T(8,128)(2,1)S(1)}, u32[]{:S(2)}, u32[]{:S(2)}) collective-permute-start(bf16[576,128]{1,0:T(8,128)(2,1)S(1)} %pad_maximum_fusion), channel_id=1, source_target_pairs={{0,16},{8,24},{16,0},{24,8},{1,17},{9,25},{17,1},{25,9},{2,18},{10... | collective-permute-start | bytes 442376 | tf_op jit(solution)/shard_map/ppermute | solution.py:27
  14.9 6.7 %collective-permute-start.5 = (bf16[576,128]{1,0:T(8,128)(2,1)S(1)}, bf16[576,128]{1,0:T(8,128)(2,1)S(1)}, u32[]{:S(2)}, u32[]{:S(2)}) collective-permute-start(bf16[576,128]{1,0:T(8,128)(2,1)S(1)} %pad_maximum_fusion), channel_id=1, source_target_pairs={{0,24},{8,0},{16,8},{24,16},{1,25},{9,1},{17,9},{25,17},{2,26},{10... | collective-permute-start | bytes 442376 | tf_op jit(solution)/shard_map/ppermute | solution.py:27
  18.0 5.8 %copy-start.1 = (f32[1024,128]{1,0:T(8,128)S(1)}, f32[1024,128]{1,0:T(8,128)}, u32[]{:S(2)}) copy-start(f32[1024,128]{1,0:T(8,128)} %gene_ref.7) | copy-start | bytes 1572868
  18.0 5.8 %copy-start.4 = (s32[48]{0:T(128)S(1)}, s32[48]{0:T(128)}, u32[]{:S(2)}) copy-start(s32[48]{0:T(128)} %rows.3) | copy-start | bytes 580
  18.0 5.8 %copy-start.5 = (s32[48]{0:T(128)S(1)}, s32[48]{0:T(128)}, u32[]{:S(2)}) copy-start(s32[48]{0:T(128)} %cols.3) | copy-start | bytes 580
  21.6 2.1 %collective-permute-start.6 = (bf16[2304,128]{1,0:T(8,128)(2,1)S(1)}, bf16[2304,128]{1,0:T(8,128)(2,1)S(1)}, u32[]{:S(2)}, u32[]{:S(2)}) collective-permute-start(bf16[2304,128]{1,0:T(8,128)(2,1)S(1)} %get-tuple-element.36), channel_id=1, source_target_pairs={{0,1},{1,0},{2,3},{3,2},{4,5},{5,4},{6,7},{7,6},{8,9},{9,8},{10,11... | collective-permute-start | bytes 1769480 | tf_op jit(solution)/shard_map/ppermute | solution.py:27
  35.2 2.0 %collective-permute-start.7 = (bf16[2048,128]{1,0:T(8,128)(2,1)S(1)}, bf16[2048,128]{1,0:T(8,128)(2,1)S(1)}, u32[]{:S(2)}, u32[]{:S(2)}) collective-permute-start(bf16[2048,128]{1,0:T(8,128)(2,1)S(1)} %get-tuple-element.11), channel_id=1, source_target_pairs={{0,1},{1,0},{2,3},{3,2},{4,5},{5,4},{6,7},{7,6},{8,9},{9,8},{10,11... | collective-permute-start | bytes 1572872 | tf_op jit(solution)/shard_map/ppermute | solution.py:27
  37.4 18.8 %copy-start.3 = (f32[128,128]{1,0:T(8,128)S(1)}, f32[128,128]{1,0:T(8,128)}, u32[]{:S(2)}) copy-start(f32[128,128]{1,0:T(8,128)} %cell_ref.3) | copy-start | bytes 196612
  37.4 9.6 %collective-permute-start.10 = (bf16[512,128]{1,0:T(8,128)(2,1)S(1)}, bf16[512,128]{1,0:T(8,128)(2,1)S(1)}, u32[]{:S(2)}, u32[]{:S(2)}) collective-permute-start(bf16[512,128]{1,0:T(8,128)(2,1)S(1)} %get-tuple-element.21), channel_id=1, source_target_pairs={{0,24},{8,0},{16,8},{24,16},{1,25},{9,1},{17,9},{25,17},{2,26},{10... | collective-permute-start | bytes 393224 | tf_op jit(solution)/shard_map/ppermute | solution.py:27
  37.5 9.5 %collective-permute-start.9 = (bf16[512,128]{1,0:T(8,128)(2,1)S(1)}, bf16[512,128]{1,0:T(8,128)(2,1)S(1)}, u32[]{:S(2)}, u32[]{:S(2)}) collective-permute-start(bf16[512,128]{1,0:T(8,128)(2,1)S(1)} %get-tuple-element.22), channel_id=1, source_target_pairs={{0,16},{8,24},{16,0},{24,8},{1,17},{9,25},{17,1},{25,9},{2,18},{10... | collective-permute-start | bytes 393224 | tf_op jit(solution)/shard_map/ppermute | solution.py:27
  38.6 9.0 %collective-permute-start.8 = (bf16[512,128]{1,0:T(8,128)(2,1)S(1)}, bf16[512,128]{1,0:T(8,128)(2,1)S(1)}, u32[]{:S(2)}, u32[]{:S(2)}) collective-permute-start(bf16[512,128]{1,0:T(8,128)(2,1)S(1)} %get-tuple-element.20), channel_id=1, source_target_pairs={{0,8},{8,16},{16,24},{24,0},{1,9},{9,17},{17,25},{25,1},{2,10},{10... | collective-permute-start | bytes 393224 | tf_op jit(solution)/shard_map/ppermute | solution.py:27
  47.8 6.8 %collective-permute-start.11 = (f32[128,128]{1,0:T(8,128)S(1)}, f32[128,128]{1,0:T(8,128)S(1)}, u32[]{:S(2)}, u32[]{:S(2)}) collective-permute-start(f32[128,128]{1,0:T(8,128)S(1)} %get-tuple-element.25), channel_id=1, source_target_pairs={{0,2},{2,4},{4,6},{6,0},{1,3},{3,5},{5,7},{7,1},{8,10},{10,12},{12... | collective-permute-start | bytes 196616 | tf_op jit(solution)/shard_map/ppermute | solution.py:27
  49.6 6.6 %collective-permute-start.12 = (f32[128,128]{1,0:T(8,128)S(1)}, f32[128,128]{1,0:T(8,128)S(1)}, u32[]{:S(2)}, u32[]{:S(2)}) collective-permute-start(f32[128,128]{1,0:T(8,128)S(1)} %get-tuple-element.24), channel_id=1, source_target_pairs={{0,4},{2,6},{4,0},{6,2},{1,5},{3,7},{5,1},{7,3},{8,12},{10,14},{12... | collective-permute-start | bytes 196616 | tf_op jit(solution)/shard_map/ppermute | solution.py:27
  49.6 6.6 %collective-permute-start.13 = (f32[128,128]{1,0:T(8,128)S(1)}, f32[128,128]{1,0:T(8,128)S(1)}, u32[]{:S(2)}, u32[]{:S(2)}) collective-permute-start(f32[128,128]{1,0:T(8,128)S(1)} %get-tuple-element.23), channel_id=1, source_target_pairs={{0,6},{2,0},{4,2},{6,4},{1,7},{3,1},{5,3},{7,5},{8,14},{10,8},{12,... | collective-permute-start | bytes 196616 | tf_op jit(solution)/shard_map/ppermute | solution.py:27
  56.8 5.8 %collective-permute-start.14 = (bf16[144,128]{1,0:T(8,128)(2,1)S(1)}, bf16[144,128]{1,0:T(8,128)(2,1)S(1)}, u32[]{:S(2)}, u32[]{:S(2)}) collective-permute-start(bf16[144,128]{1,0:T(8,128)(2,1)S(1)} %get-tuple-element.14), channel_id=1, source_target_pairs={{0,2},{2,4},{4,6},{6,0},{1,3},{3,5},{5,7},{7,1},{8,10},{10,12},{12... | collective-permute-start | bytes 110600 | tf_op jit(solution)/shard_map/ppermute | solution.py:27
  58.1 5.3 %collective-permute-start.15 = (bf16[144,128]{1,0:T(8,128)(2,1)S(1)}, bf16[144,128]{1,0:T(8,128)(2,1)S(1)}, u32[]{:S(2)}, u32[]{:S(2)}) collective-permute-start(bf16[144,128]{1,0:T(8,128)(2,1)S(1)} %get-tuple-element.14), channel_id=1, source_target_pairs={{0,4},{2,6},{4,0},{6,2},{1,5},{3,7},{5,1},{7,3},{8,12},{10,14},{12... | collective-permute-start | bytes 110600 | tf_op jit(solution)/shard_map/ppermute | solution.py:27
  60.0 4.0 %collective-permute-start.16 = (bf16[144,128]{1,0:T(8,128)(2,1)S(1)}, bf16[144,128]{1,0:T(8,128)(2,1)S(1)}, u32[]{:S(2)}, u32[]{:S(2)}) collective-permute-start(bf16[144,128]{1,0:T(8,128)(2,1)S(1)} %get-tuple-element.14), channel_id=1, source_target_pairs={{0,6},{2,0},{4,2},{6,4},{1,7},{3,1},{5,3},{7,5},{8,14},{10,8},{12,... | collective-permute-start | bytes 110600 | tf_op jit(solution)/shard_map/ppermute | solution.py:27
  63.9 8.3 %collective-permute-start.17 = (bf16[576,128]{1,0:T(8,128)(2,1)S(1)}, bf16[576,128]{1,0:T(8,128)(2,1)S(1)}, u32[]{:S(2)}, u32[]{:S(2)}) collective-permute-start(bf16[576,128]{1,0:T(8,128)(2,1)S(1)} %get-tuple-element.44), channel_id=1, source_target_pairs={{0,8},{8,16},{16,24},{24,0},{1,9},{9,17},{17,25},{25,1},{2,10},{10... | collective-permute-start | bytes 442376 | tf_op jit(solution)/shard_map/ppermute | solution.py:27
  66.9 7.6 %collective-permute-start.18 = (bf16[576,128]{1,0:T(8,128)(2,1)S(1)}, bf16[576,128]{1,0:T(8,128)(2,1)S(1)}, u32[]{:S(2)}, u32[]{:S(2)}) collective-permute-start(bf16[576,128]{1,0:T(8,128)(2,1)S(1)} %get-tuple-element.44), channel_id=1, source_target_pairs={{0,16},{8,24},{16,0},{24,8},{1,17},{9,25},{17,1},{25,9},{2,18},{10... | collective-permute-start | bytes 442376 | tf_op jit(solution)/shard_map/ppermute | solution.py:27
  66.9 8.8 %collective-permute-start.19 = (bf16[576,128]{1,0:T(8,128)(2,1)S(1)}, bf16[576,128]{1,0:T(8,128)(2,1)S(1)}, u32[]{:S(2)}, u32[]{:S(2)}) collective-permute-start(bf16[576,128]{1,0:T(8,128)(2,1)S(1)} %get-tuple-element.44), channel_id=1, source_target_pairs={{0,24},{8,0},{16,8},{24,16},{1,25},{9,1},{17,9},{25,17},{2,26},{10... | collective-permute-start | bytes 442376 | tf_op jit(solution)/shard_map/ppermute | solution.py:27
  75.8 2.1 %collective-permute-start.20 = (bf16[2304,128]{1,0:T(8,128)(2,1)S(1)}, bf16[2304,128]{1,0:T(8,128)(2,1)S(1)}, u32[]{:S(2)}, u32[]{:S(2)}) collective-permute-start(bf16[2304,128]{1,0:T(8,128)(2,1)S(1)} %get-tuple-element.30), channel_id=1, source_target_pairs={{0,1},{1,0},{2,3},{3,2},{4,5},{5,4},{6,7},{7,6},{8,9},{9,8},{10,11... | collective-permute-start | bytes 1769480 | tf_op jit(solution)/shard_map/ppermute | solution.py:27
  91.3 5.6 %collective-permute-start.21 = (bf16[272,128]{1,0:T(8,128)(2,1)S(1)}, bf16[272,128]{1,0:T(8,128)(2,1)S(1)}, u32[]{:S(2)}, u32[]{:S(2)}) collective-permute-start(bf16[272,128]{1,0:T(8,128)(2,1)S(1)} %get-tuple-element.29), channel_id=1, source_target_pairs={{0,64},{64,128},{128,192},{192,0},{1,65},{65,129},{129,193},{193,1... | collective-permute-start | bytes 208904 | tf_op jit(solution)/shard_map/ppermute | solution.py:27
  91.4 8.8 %collective-permute-start.22 = (bf16[272,128]{1,0:T(8,128)(2,1)S(1)}, bf16[272,128]{1,0:T(8,128)(2,1)S(1)}, u32[]{:S(2)}, u32[]{:S(2)}) collective-permute-start(bf16[272,128]{1,0:T(8,128)(2,1)S(1)} %get-tuple-element.28), channel_id=1, source_target_pairs={{0,128},{64,192},{128,0},{192,64},{1,129},{65,193},{129,1},{193,65... | collective-permute-start | bytes 208904 | tf_op jit(solution)/shard_map/ppermute | solution.py:27
  95.8 4.5 %collective-permute-start.23 = (bf16[272,128]{1,0:T(8,128)(2,1)S(1)}, bf16[272,128]{1,0:T(8,128)(2,1)S(1)}, u32[]{:S(2)}, u32[]{:S(2)}) collective-permute-start(bf16[272,128]{1,0:T(8,128)(2,1)S(1)} %get-tuple-element.27), channel_id=1, source_target_pairs={{0,192},{64,0},{128,64},{192,128},{1,193},{65,1},{129,65},{193,129... | collective-permute-start | bytes 208904 | tf_op jit(solution)/shard_map/ppermute | solution.py:27
  100.3 10.9 %collective-permute-start.24 = (f32[264,128]{1,0:T(8,128)S(1)}, f32[264,128]{1,0:T(8,128)S(1)}, u32[]{:S(2)}, u32[]{:S(2)}) collective-permute-start(f32[264,128]{1,0:T(8,128)S(1)} %fold.1.mine_ref), channel_id=1, source_target_pairs={{0,32},{32,0},{1,33},{33,1},{2,34},{34,2},{3,35},{35,3},{4,36},{36... | collective-permute-start | bytes 405512 | tf_op jit(solution)/shard_map/ppermute | solution.py:27
  111.8 6.4 %collective-permute-start.25 = (f32[256,128]{1,0:T(8,128)S(1)}, f32[256,128]{1,0:T(8,128)S(1)}, u32[]{:S(2)}, u32[]{:S(2)}) collective-permute-start(f32[256,128]{1,0:T(8,128)S(1)} %finish.1.p0_ref), channel_id=1, source_target_pairs={{0,64},{64,128},{128,192},{192,0},{1,65},{65,129},{129,193},{193,1... | collective-permute-start | bytes 393224 | tf_op jit(solution)/shard_map/ppermute | solution.py:27
  112.4 9.7 %collective-permute-start.26 = (f32[256,128]{1,0:T(8,128)S(1)}, f32[256,128]{1,0:T(8,128)S(1)}, u32[]{:S(2)}, u32[]{:S(2)}) collective-permute-start(f32[256,128]{1,0:T(8,128)S(1)} %finish.1.p0_ref), channel_id=1, source_target_pairs={{0,128},{64,192},{128,0},{192,64},{1,129},{65,193},{129,1},{193,65... | collective-permute-start | bytes 393224 | tf_op jit(solution)/shard_map/ppermute | solution.py:27
  115.9 6.3 %collective-permute-start.27 = (f32[256,128]{1,0:T(8,128)S(1)}, f32[256,128]{1,0:T(8,128)S(1)}, u32[]{:S(2)}, u32[]{:S(2)}) collective-permute-start(f32[256,128]{1,0:T(8,128)S(1)} %finish.1.p0_ref), channel_id=1, source_target_pairs={{0,192},{64,0},{128,64},{192,128},{1,193},{65,1},{129,65},{193,129... | collective-permute-start | bytes 393224 | tf_op jit(solution)/shard_map/ppermute | solution.py:27

commit v2 on v1

v2 whole, which is shorter than its diff:
```python
import jax
import jax.numpy as jnp
from jax import lax
from jax.experimental import pallas as pl
from jax.experimental.pallas import tpu as pltpu
from jax.sharding import Mesh
from jax.sharding import PartitionSpec as P

GENE = ("x", "zl", "c")
CELL_GENE = ("y", "zh", "x", "zl", "c")

BLK = 256
R = 128
NB = 48
HALF = 128
PAD = 144
UNITS = 32
GROUP = 16
BF = jnp.bfloat16
F32 = jnp.float32
NT = (((1,), (1,)), ((), ()))
TN = (((0,), (0,)), ((), ()))
VMEM_LIMIT = 24 * 1024 * 1024


SHIFTED = ('zl', 'y')


def partner(axis, i, step):
    return i + step if axis in SHIFTED else i ^ step


def swap(value, axis, step):
    count = lax.axis_size(axis)
    return lax.ppermute(value, axis, [(i, partner(axis, i, step) % count) for i in range(count)])


def gathered(payload):
    for axis in ("zl", "x", "c"):
        parts = [payload] + [swap(payload, axis, k) for k in range(1, lax.axis_size(axis))]
        payload = jnp.concatenate(parts, 0)
    return payload


def three_pieces(total):
    hi = total.astype(BF)
    rest = total - hi.astype(F32)
    mid = rest.astype(BF)
    lo = (rest - mid.astype(F32)).astype(BF)
    wide = lambda a: jnp.concatenate([a.astype(F32)] * 2, 0)
    which = lax.broadcasted_iota(jnp.int32, (16, R), 0)
    rows = jnp.where(
        which == 0,
        wide(hi),
        jnp.where(which == 1, wide(mid), jnp.where(which == 2, wide(lo), 0.0)),
    )
    return rows.astype(BF)


def column_sum(value):
    return jnp.broadcast_to(jnp.sum(value, 0, keepdims=True), (8, R))


def prep_kernel(cell_ref, gene_ref, pay_ref, hb_ref, cell, gene, sems):
    copies = [
        pltpu.make_async_copy(gene_ref, gene, sems.at[0]),
        pltpu.make_async_copy(cell_ref, cell, sems.at[1]),
    ]
    for copy in copies:
        copy.start()
    for copy in copies:
        copy.wait()
    pay_ref[:HALF, :] = cell[...].astype(BF)
    pay_ref[HALF:, :] = three_pieces(column_sum(gene[...]))
    hb_ref[...] = gene[...].astype(BF)


def slot_base(meta, row, other):
    dx = meta[0] ^ (row >> 2)
    dz = (meta[1] - (row & 3)) & 3
    return pl.multiple_of((other * 16 + dx * 4 + dz) * PAD, 16)


def unit_base(meta, row):
    dx = meta[0] ^ (row >> 2)
    dz = ((row & 3) - meta[1]) & 3
    return pl.multiple_of((dx * 4 + dz) * HALF, HALF)


def group_sum(g_ref):
    total = jnp.zeros((16, R), F32)
    for u in range(UNITS):
        total = total + g_ref[u * PAD + HALF : (u + 1) * PAD, :].astype(F32)
    return column_sum(total)


def ratio_of(tile, w, h, live):
    model = lax.dot_general(w, h, NT, preferred_element_type=F32)
    return jnp.where(live, tile.astype(F32) / model, 0.0).astype(BF)


def cells_kernel(
    meta, rows, cols, blocks_ref, g_ref, hb_ref, keep_ref, send_ref, sum_ref, acc, tiles, sems
):
    def batch(p):
        at = pl.ds(p * GROUP, GROUP)
        return pltpu.make_async_copy(blocks_ref.at[at], tiles.at[at], sems.at[p])

    for p in range(NB // GROUP):
        batch(p).start()
    keep_ref[...] = jnp.zeros_like(keep_ref)
    acc[...] = jnp.zeros_like(acc)
    sum_ref[...] = group_sum(g_ref)
    count = meta[3]

    def step(p, carry):
        batch(p).wait()
        found = []
        for k in range(GROUP):
            s = p * GROUP + k
            row = rows[s]
            h = hb_ref[pl.ds(pl.multiple_of(cols[s] * BLK, BLK), BLK), :]
            terms = []
            for other in (0, 1):
                w = g_ref[pl.ds(slot_base(meta, row, other), HALF), :]
                at = pl.multiple_of((meta[2] ^ other) * HALF, HALF)
                ratio = ratio_of(tiles[s, pl.ds(at, HALF), :], w, h, s < count)
                terms.append(jnp.dot(ratio, h, preferred_element_type=F32))
            found.append((unit_base(meta, row), terms))
        for at, terms in found:
            at = pl.ds(at, HALF)
            keep_ref[at, :] = keep_ref[at, :] + terms[0]
            acc[at, :] = acc[at, :] + terms[1]
        return carry

    steps = (count + GROUP - 1) // GROUP
    lax.fori_loop(0, steps, step, 0)
    send_ref[...] = acc[...].astype(BF)

    def drain(p, carry):
        batch(p).wait()
        return carry

    lax.fori_loop(steps, NB // GROUP, drain, 0)


def update_kernel(own_ref, r1_ref, r2_ref, r3_ref, cell_ref, sum_ref, new_ref, pay_ref):
    numer = own_ref[...] + r1_ref[...] + r2_ref[...] + r3_ref[...]
    new = cell_ref[...] * numer / sum_ref[0:1, :]
    new_ref[...] = new
    pay_ref[:HALF, :] = new.astype(BF)
    pay_ref[HALF:, :] = three_pieces(column_sum(new))


def genes_kernel(
    meta, rows, cols, blocks_ref, g_ref, hb_ref, own_ref, s1_ref, s2_ref, s3_ref, acc
):
    acc[...] = jnp.zeros_like(acc)
    total = group_sum(g_ref)
    count = meta[3]

    def step(p, carry):
        found = []
        for k in range(GROUP):
            s = p * GROUP + k
            row = rows[s]
            h = hb_ref[pl.ds(pl.multiple_of(cols[s] * BLK, BLK), BLK), :]
            w = jnp.concatenate(
                [
                    g_ref[pl.ds(slot_base(meta, row, meta[2] ^ parity), HALF), :]
                    for parity in (0, 1)
                ],
                0,
            )
            ratio = ratio_of(blocks_ref[s], w, h, s < count)
            found.append(
                (
                    (cols[s] - meta[4]) & 3,
                    lax.dot_general(ratio, w, TN, preferred_element_type=F32),
                )
            )
        for at, terms in found:
            acc[at] = acc[at] + terms
        return carry

    lax.fori_loop(0, (count + GROUP - 1) // GROUP, step, 0)
    for k, ref in enumerate((own_ref, s1_ref, s2_ref, s3_ref)):
        ref[:BLK, :] = acc[k]
        ref[BLK:, :] = total


def fold_kernel(own_ref, r1_ref, r2_ref, r3_ref, out_ref):
    out_ref[...] = own_ref[...] + r1_ref[...] + r2_ref[...] + r3_ref[...]


def finish_kernel(meta, mine_ref, other_ref, gene_ref, out_ref):
    both = mine_ref[...] + other_ref[...]
    at = pl.ds(pl.multiple_of(meta[4] * BLK, BLK), BLK)
    out_ref[...] = gene_ref[at, :] * both[:BLK] / both[BLK : BLK + 1]


def place_kernel(meta, p0_ref, p1_ref, p2_ref, p3_ref, out_ref, sems):
    copies = []
    for k, ref in enumerate((p0_ref, p1_ref, p2_ref, p3_ref)):
        at = pl.ds(pl.multiple_of(((meta[4] - k) & 3) * BLK, BLK), BLK)
        copies.append(pltpu.make_async_copy(ref, out_ref.at[at, :], sems.at[k]))
    for copy in copies:
        copy.start()
    for copy in copies:
        copy.wait()


def vspec():
    return pl.BlockSpec(memory_space=pltpu.VMEM)


def sspec():
    return pl.BlockSpec(memory_space=pltpu.SMEM)


def call(kernel, outs, args, kinds, gives="", scratch=(), name=None):
    spec = {"s": sspec, "v": vspec, "a": lambda: pl.BlockSpec(memory_space=pl.ANY)}
    kept = [spec[kind]() for kind in gives or "v" * len(jax.tree.leaves(outs))]
    return pl.pallas_call(
        kernel,
        out_shape=outs,
        in_specs=[spec[kind]() for kind in kinds],
        out_specs=tuple(kept) if isinstance(outs, tuple) else kept[0],
        scratch_shapes=list(scratch),
        name=name,
        compiler_params=pltpu.CompilerParams(vmem_limit_bytes=VMEM_LIMIT),
    )(*args)


def in_hbm(value):
    return pltpu.with_memory_space_constraint(value, pltpu.HBM)


def shape(dims, dtype):
    return jax.ShapeDtypeStruct(dims, dtype)


def on_device(blocks, block_rows, block_cols, block_count, cell_factor, gene_factor):
    genes = gene_factor.shape[0]
    half = UNITS // 2 * HALF
    meta = jnp.stack(
        [
            lax.axis_index("x"),
            lax.axis_index("zl"),
            lax.axis_index("c"),
            block_count[0],
            lax.axis_index("y"),
        ]
    ).astype(jnp.int32)
    pay, hb = call(
        prep_kernel,
        (shape((PAD, R), BF), shape((genes, R), BF)),
        (in_hbm(cell_factor), in_hbm(gene_factor)),
        "aa",
        scratch=[
            pltpu.VMEM((HALF, R), F32),
            pltpu.VMEM((genes, R), F32),
            pltpu.SemaphoreType.DMA((2,)),
        ],
        name="prep",
    )
    g1 = gathered(pay)
    keep, send, gene_sums = call(
        cells_kernel,
        (shape((half, R), F32), shape((half, R), BF), shape((8, R), F32)),
        (meta, block_rows, block_cols, in_hbm(blocks), g1, hb),
        "sssavv",
        scratch=[
            pltpu.VMEM((half, R), F32),
            pltpu.VMEM((NB, BLK, BLK), BF),
            pltpu.SemaphoreType.DMA((NB // GROUP,)),
        ],
        name="cells",
    )
    part = keep + swap(send, "c", 1).astype(F32)
    quarter = half // 4
    sent = [swap(part[k * quarter : (k + 1) * quarter].astype(BF), "x", k) for k in (1, 2, 3)]
    part = part[:quarter]
    for arrived in sent:
        part = part + arrived.astype(F32)
    own = part[:HALF]
    sent = [swap(part[k * HALF : (k + 1) * HALF], "zl", k) for k in (1, 2, 3)]
    cell_new, pay = call(
        update_kernel,
        (shape((HALF, R), F32), shape((PAD, R), BF)),
        (own, *sent, cell_factor, gene_sums),
        "vvvvvv",
        name="update",
    )
    g2 = gathered(pay)
    mine, *send = call(
        genes_kernel,
        (shape((BLK + 8, R), F32),) * 4,
        (meta, block_rows, block_cols, blocks, g2, hb),
        "sssvvv",
        scratch=[pltpu.VMEM((4, BLK, R), F32)],
        name="genes",
    )
    arrived = [swap(send[k - 1], "y", k) for k in (1, 2, 3)]
    folded = call(fold_kernel, shape((BLK + 8, R), F32), (mine, *arrived), "vvvv", name="fold")
    other = swap(folded, "zh", 1)
    fresh = call(
        finish_kernel,
        shape((BLK, R), F32),
        (meta, folded, other, gene_factor),
        "svvv",
        name="finish",
    )
    parts = [fresh] + [swap(fresh, "y", k) for k in (1, 2, 3)]
    gene_new = call(
        place_kernel,
        shape((genes, R), F32),
        (meta, *parts),
        "svvvv",
        gives="a",
        scratch=[pltpu.SemaphoreType.DMA((4,))],
        name="place",
    )
    return (cell_new, gene_new)


def solution(mesh):
    torus = Mesh(mesh.devices.reshape(4, 2, 4, 4, 2), CELL_GENE)
    return jax.shard_map(
        on_device,
        mesh=torus,
        in_specs=(
            P(CELL_GENE, None, None),
            P(CELL_GENE),
            P(CELL_GENE),
            P(CELL_GENE),
            P(CELL_GENE, None),
            P(GENE, None),
        ),
        out_specs=(P(CELL_GENE, None), P(GENE, None)),
        check_vma=False,
    )
```

time: 122 us -> 111 us (0.910)
  the two profiles are of different devices: /device:TPU:6 before, /device:TPU:1 now
where the time goes in v2:
time: 111 us; the launch traced here: 112 us
  starting transfers between devices  53.3 us (48%)
  waiting for transfers between devices  45.3 us (41%)
  Pallas kernels  10.3 us (9%)
  between operations  1.69 us (2%)
    ppermute x28, starting transfers between devices, swap(): lax.ppermute(value, axis, [(i, partner(axis, i, step) % count) for i in r...  53.3 us
    ppermute x28, waiting for transfers between devices, swap(): lax.ppermute(value, axis, [(i, partner(axis, i, step) % count) for i in r...  45.3 us
    pallas_call x7, Pallas kernels, call(): pl.pallas_call(kernel, out_shape=outs, in_specs=[spec[kind]() for kind in...  10.3 us
  transfers between devices with their start and end apart: 28, of which 24 were waited for; matrix products, arithmetic and copies ran while one was open for 0% of the time, Pallas kernels for 0%

profile of v2, /device:TPU:1, one launch (start us, length us, event | category | flops | bytes accessed | tf_op | source)
XLA Modules:
  0.0 111.5 jit_solution(11579367396866951233)
XLA Ops:
  0.6 1.2 %prep.1 = (bf16[144,128]{1,0:T(8,128)(2,1)S(1)}, bf16[1024,128]{1,0:T(8,128)(2,1)S(1)}) custom-call(f32[128,128]{1,0:T(8,128)} %cell_ref.3, f32[1024,128]{1,0:T(8,128)} %gene_ref.3), custom_call_target="tpu_custom_call" | custom-call | tf_op jit(solution)/shard_map/prep/pallas_call | solution.py:224
  1.9 2.5 %collective-permute-start = (bf16[144,128]{1,0:T(8,128)(2,1)S(1)}, bf16[144,128]{1,0:T(8,128)(2,1)S(1)}, u32[]{:S(2)}, u32[]{:S(2)}) collective-permute-start(bf16[144,128]{1,0:T(8,128)(2,1)S(1)} %get-tuple-element.13), channel_id=1, source_target_pairs={{0,2},{2,4},{4,6},{6,0},{1,3},{3,5},{5,7},{7,1},{8,10},{10,12},{12... | collective-permute-start | bytes 110600 | tf_op jit(solution)/shard_map/ppermute | solution.py:35
  4.4 3.0 %collective-permute-start.1 = (bf16[144,128]{1,0:T(8,128)(2,1)S(1)}, bf16[144,128]{1,0:T(8,128)(2,1)S(1)}, u32[]{:S(2)}, u32[]{:S(2)}) collective-permute-start(bf16[144,128]{1,0:T(8,128)(2,1)S(1)} %get-tuple-element.13), channel_id=1, source_target_pairs={{0,4},{2,6},{4,0},{6,2},{1,5},{3,7},{5,1},{7,3},{8,12},{10,14},{12... | collective-permute-start | bytes 110600 | tf_op jit(solution)/shard_map/ppermute | solution.py:35
  7.4 0.7 collective-permute-start.2
  8.1 0.3 collective-permute-done
  8.5 0.4 collective-permute-done.1
  8.9 2.2 %collective-permute-done.2 = bf16[144,128]{1,0:T(8,128)(2,1)S(1)} collective-permute-done((bf16[144,128]{1,0:T(8,128)(2,1)S(1)}, bf16[144,128]{1,0:T(8,128)(2,1)S(1)}, u32[]{:S(2)}, u32[]{:S(2)}) %collective-permute-start.2) | collective-permute-done | bytes 36896 | tf_op jit(solution)/shard_map/ppermute | solution.py:35
  11.1 1.0 collective-permute-start.3
  12.1 2.5 %collective-permute-start.4 = (bf16[576,128]{1,0:T(8,128)(2,1)S(1)}, bf16[576,128]{1,0:T(8,128)(2,1)S(1)}, u32[]{:S(2)}, u32[]{:S(2)}) collective-permute-start(bf16[576,128]{1,0:T(8,128)(2,1)S(1)} %get-tuple-element.59), channel_id=1, source_target_pairs={{0,16},{8,24},{16,0},{24,8},{1,17},{9,25},{17,1},{25,9},{2,18},{10... | collective-permute-start | bytes 442376 | tf_op jit(solution)/shard_map/ppermute | solution.py:35
  14.5 0.5 collective-permute-start.5
  15.2 4.3 %collective-permute-done.4 = bf16[576,128]{1,0:T(8,128)(2,1)S(1)} collective-permute-done((bf16[576,128]{1,0:T(8,128)(2,1)S(1)}, bf16[576,128]{1,0:T(8,128)(2,1)S(1)}, u32[]{:S(2)}, u32[]{:S(2)}) %collective-permute-start.4) | collective-permute-done | bytes 147488 | tf_op jit(solution)/shard_map/ppermute | solution.py:35
  19.5 2.8 %collective-permute-done.5 = bf16[576,128]{1,0:T(8,128)(2,1)S(1)} collective-permute-done((bf16[576,128]{1,0:T(8,128)(2,1)S(1)}, bf16[576,128]{1,0:T(8,128)(2,1)S(1)}, u32[]{:S(2)}, u32[]{:S(2)}) %collective-permute-start.5) | collective-permute-done | bytes 147488 | tf_op jit(solution)/shard_map/ppermute | solution.py:35
  22.3 2.1 %collective-permute-start.6 = (bf16[2304,128]{1,0:T(8,128)(2,1)S(1)}, bf16[2304,128]{1,0:T(8,128)(2,1)S(1)}, u32[]{:S(2)}, u32[]{:S(2)}) collective-permute-start(bf16[2304,128]{1,0:T(8,128)(2,1)S(1)} %get-tuple-element.39), channel_id=1, source_target_pairs={{0,1},{1,0},{2,3},{3,2},{4,5},{5,4},{6,7},{7,6},{8,9},{9,8},{10,11... | collective-permute-start | bytes 1769480 | tf_op jit(solution)/shard_map/ppermute | solution.py:35
  25.1 0.9 collective-permute-done.6
  26.1 4.1 %cells.1 = (f32[2048,128]{1,0:T(8,128)S(1)}, bf16[2048,128]{1,0:T(8,128)(2,1)S(1)}, f32[8,128]{1,0:T(8,128)S(1)}) custom-call(s32[5]{0:T(128)S(1)} %stack.19.meta, s32[48]{0:T(128)S(1)} %copy-done.2, s32[48]{0:T(128)S(1)} %copy-done.3, bf16[48,256,256]{2,1,0:T(8,128)(2,1)} %blocks_ref.3, bf16[4608,128]{1,0:T(8,128)(2,1)S(1)} %constant_dynamic-update-slice_fusion.11.g_ref, ...), custom_call_target="tpu_custom_call" | custom-call | tf_op jit(solution)/shard_map/cells/pallas_call | solution.py:224
  30.2 3.5 %collective-permute-start.7 = (bf16[2048,128]{1,0:T(8,128)(2,1)S(1)}, bf16[2048,128]{1,0:T(8,128)(2,1)S(1)}, u32[]{:S(2)}, u32[]{:S(2)}) collective-permute-start(bf16[2048,128]{1,0:T(8,128)(2,1)S(1)} %get-tuple-element.16), channel_id=1, source_target_pairs={{0,1},{1,0},{2,3},{3,2},{4,5},{5,4},{6,7},{7,6},{8,9},{9,8},{10,11... | collective-permute-start | bytes 1572872 | tf_op jit(solution)/shard_map/ppermute | solution.py:35
  33.7 1.5 %collective-permute-done.7 = bf16[2048,128]{1,0:T(8,128)(2,1)S(1)} collective-permute-done((bf16[2048,128]{1,0:T(8,128)(2,1)S(1)}, bf16[2048,128]{1,0:T(8,128)(2,1)S(1)}, u32[]{:S(2)}, u32[]{:S(2)}) %collective-permute-start.7) | collective-permute-done | bytes 524320 | tf_op jit(solution)/shard_map/ppermute | solution.py:35
  35.4 1.0 collective-permute-start.10
  36.4 2.3 %collective-permute-start.8 = (bf16[512,128]{1,0:T(8,128)(2,1)S(1)}, bf16[512,128]{1,0:T(8,128)(2,1)S(1)}, u32[]{:S(2)}, u32[]{:S(2)}) collective-permute-start(bf16[512,128]{1,0:T(8,128)(2,1)S(1)} %get-tuple-element.26), channel_id=1, source_target_pairs={{0,8},{8,0},{16,24},{24,16},{1,9},{9,1},{17,25},{25,17},{2,10},{10... | collective-permute-start | bytes 393224 | tf_op jit(solution)/shard_map/ppermute | solution.py:35
  38.8 5.1 %collective-permute-done.10 = bf16[512,128]{1,0:T(8,128)(2,1)S(1)} collective-permute-done((bf16[512,128]{1,0:T(8,128)(2,1)S(1)}, bf16[512,128]{1,0:T(8,128)(2,1)S(1)}, u32[]{:S(2)}, u32[]{:S(2)}) %collective-permute-start.10) | collective-permute-done | bytes 131104 | tf_op jit(solution)/shard_map/ppermute | solution.py:35
  43.9 0.7 collective-permute-done.8
  44.8 0.5 collective-permute-start.12
  45.3 2.7 %collective-permute-start.13 = (f32[128,128]{1,0:T(8,128)S(1)}, f32[128,128]{1,0:T(8,128)S(1)}, u32[]{:S(2)}, u32[]{:S(2)}) collective-permute-start(f32[128,128]{1,0:T(8,128)S(1)} %get-tuple-element.29), channel_id=1, source_target_pairs={{0,6},{2,0},{4,2},{6,4},{1,7},{3,1},{5,3},{7,5},{8,14},{10,8},{12,... | collective-permute-start | bytes 196616 | tf_op jit(solution)/shard_map/ppermute | solution.py:35
  48.0 1.7 %collective-permute-done.11.r1_ref = f32[128,128]{1,0:T(8,128)S(1)} collective-permute-done((f32[128,128]{1,0:T(8,128)S(1)}, f32[128,128]{1,0:T(8,128)S(1)}, u32[]{:S(2)}, u32[]{:S(2)}) %collective-permute-start.11) | collective-permute-done | bytes 65568 | tf_op jit(solution)/shard_map/ppermute | solution.py:35
  49.7 1.0 collective-permute-done.13.r3_ref
  50.7 0.7 update.1
  51.4 3.1 %collective-permute-start.14 = (bf16[144,128]{1,0:T(8,128)(2,1)S(1)}, bf16[144,128]{1,0:T(8,128)(2,1)S(1)}, u32[]{:S(2)}, u32[]{:S(2)}) collective-permute-start(bf16[144,128]{1,0:T(8,128)(2,1)S(1)} %get-tuple-element.19), channel_id=1, source_target_pairs={{0,2},{2,4},{4,6},{6,0},{1,3},{3,5},{5,7},{7,1},{8,10},{10,12},{12... | collective-permute-start | bytes 110600 | tf_op jit(solution)/shard_map/ppermute | solution.py:35
  54.5 0.3 collective-permute-start.15
  54.8 2.1 %collective-permute-start.16 = (bf16[144,128]{1,0:T(8,128)(2,1)S(1)}, bf16[144,128]{1,0:T(8,128)(2,1)S(1)}, u32[]{:S(2)}, u32[]{:S(2)}) collective-permute-start(bf16[144,128]{1,0:T(8,128)(2,1)S(1)} %get-tuple-element.19), channel_id=1, source_target_pairs={{0,6},{2,0},{4,2},{6,4},{1,7},{3,1},{5,3},{7,5},{8,14},{10,8},{12,... | collective-permute-start | bytes 110600 | tf_op jit(solution)/shard_map/ppermute | solution.py:35
  56.9 1.7 %collective-permute-done.15 = bf16[144,128]{1,0:T(8,128)(2,1)S(1)} collective-permute-done((bf16[144,128]{1,0:T(8,128)(2,1)S(1)}, bf16[144,128]{1,0:T(8,128)(2,1)S(1)}, u32[]{:S(2)}, u32[]{:S(2)}) %collective-permute-start.15) | collective-permute-done | bytes 36896 | tf_op jit(solution)/shard_map/ppermute | solution.py:35
  58.7 2.1 %collective-permute-start.18 = (bf16[576,128]{1,0:T(8,128)(2,1)S(1)}, bf16[576,128]{1,0:T(8,128)(2,1)S(1)}, u32[]{:S(2)}, u32[]{:S(2)}) collective-permute-start(bf16[576,128]{1,0:T(8,128)(2,1)S(1)} %get-tuple-element.47), channel_id=1, source_target_pairs={{0,16},{8,24},{16,0},{24,8},{1,17},{9,25},{17,1},{25,9},{2,18},{10... | collective-permute-start | bytes 442376 | tf_op jit(solution)/shard_map/ppermute | solution.py:35
  60.8 1.8 %collective-permute-start.19 = (bf16[576,128]{1,0:T(8,128)(2,1)S(1)}, bf16[576,128]{1,0:T(8,128)(2,1)S(1)}, u32[]{:S(2)}, u32[]{:S(2)}) collective-permute-start(bf16[576,128]{1,0:T(8,128)(2,1)S(1)} %get-tuple-element.47), channel_id=1, source_target_pairs={{0,24},{8,16},{16,8},{24,0},{1,25},{9,17},{17,9},{25,1},{2,26},{10... | collective-permute-start | bytes 442376 | tf_op jit(solution)/shard_map/ppermute | solution.py:35
  62.8 2.2 %collective-permute-done.18 = bf16[576,128]{1,0:T(8,128)(2,1)S(1)} collective-permute-done((bf16[576,128]{1,0:T(8,128)(2,1)S(1)}, bf16[576,128]{1,0:T(8,128)(2,1)S(1)}, u32[]{:S(2)}, u32[]{:S(2)}) %collective-permute-start.18) | collective-permute-done | bytes 147488 | tf_op jit(solution)/shard_map/ppermute | solution.py:35
  65.0 1.5 %collective-permute-done.19 = bf16[576,128]{1,0:T(8,128)(2,1)S(1)} collective-permute-done((bf16[576,128]{1,0:T(8,128)(2,1)S(1)}, bf16[576,128]{1,0:T(8,128)(2,1)S(1)}, u32[]{:S(2)}, u32[]{:S(2)}) %collective-permute-start.19) | collective-permute-done | bytes 147488 | tf_op jit(solution)/shard_map/ppermute | solution.py:35
  66.6 4.4 %collective-permute-start.20 = (bf16[2304,128]{1,0:T(8,128)(2,1)S(1)}, bf16[2304,128]{1,0:T(8,128)(2,1)S(1)}, u32[]{:S(2)}, u32[]{:S(2)}) collective-permute-start(bf16[2304,128]{1,0:T(8,128)(2,1)S(1)} %get-tuple-element.33), channel_id=1, source_target_pairs={{0,1},{1,0},{2,3},{3,2},{4,5},{5,4},{6,7},{7,6},{8,9},{9,8},{10,11... | collective-permute-start | bytes 1769480 | tf_op jit(solution)/shard_map/ppermute | solution.py:35
  71.0 1.6 %collective-permute-done.20 = bf16[2304,128]{1,0:T(8,128)(2,1)S(1)} collective-permute-done((bf16[2304,128]{1,0:T(8,128)(2,1)S(1)}, bf16[2304,128]{1,0:T(8,128)(2,1)S(1)}, u32[]{:S(2)}, u32[]{:S(2)}) %collective-permute-start.20) | collective-permute-done | bytes 589856 | tf_op jit(solution)/shard_map/ppermute | solution.py:35
  72.7 2.4 %genes.1 = (f32[264,128]{1,0:T(8,128)S(1)}, f32[264,128]{1,0:T(8,128)S(1)}, f32[264,128]{1,0:T(8,128)S(1)}, f32[264,128]{1,0:T(8,128)S(1)}) custom-call(s32[5]{0:T(128)S(1)} %stack.19.meta, s32[48]{0:T(128)S(1)} %copy-done.2, s32[48]{0:T(128)S(1)} %copy-done.3, bf16[48,256,256]{2,1,0:T(8,128)(2,1)S(1)} %bitcast.5, ...), custom_call_target="tpu_custom_call" | custom-call | tf_op jit(solution)/shard_map/genes/pallas_call | solution.py:224
  75.2 7.0 %collective-permute-start.22 = (f32[264,128]{1,0:T(8,128)S(1)}, f32[264,128]{1,0:T(8,128)S(1)}, u32[]{:S(2)}, u32[]{:S(2)}) collective-permute-start(f32[264,128]{1,0:T(8,128)S(1)} %get-tuple-element.22), channel_id=1, source_target_pairs={{0,128},{64,192},{128,0},{192,64},{1,129},{65,193},{129,1},{193,65... | collective-permute-start | bytes 405512 | tf_op jit(solution)/shard_map/ppermute | solution.py:35
  82.2 2.1 %collective-permute-done.21.r1_ref = f32[264,128]{1,0:T(8,128)S(1)} collective-permute-done((f32[264,128]{1,0:T(8,128)S(1)}, f32[264,128]{1,0:T(8,128)S(1)}, u32[]{:S(2)}, u32[]{:S(2)}) %collective-permute-start.21) | collective-permute-done | bytes 135200 | tf_op jit(solution)/shard_map/ppermute | solution.py:35
  84.3 3.2 %collective-permute-done.22.r2_ref = f32[264,128]{1,0:T(8,128)S(1)} collective-permute-done((f32[264,128]{1,0:T(8,128)S(1)}, f32[264,128]{1,0:T(8,128)S(1)}, u32[]{:S(2)}, u32[]{:S(2)}) %collective-permute-start.22) | collective-permute-done | bytes 135200 | tf_op jit(solution)/shard_map/ppermute | solution.py:35
  87.8 2.5 %collective-permute-start.24 = (f32[264,128]{1,0:T(8,128)S(1)}, f32[264,128]{1,0:T(8,128)S(1)}, u32[]{:S(2)}, u32[]{:S(2)}) collective-permute-start(f32[264,128]{1,0:T(8,128)S(1)} %fold.1.mine_ref), channel_id=1, source_target_pairs={{0,32},{32,0},{1,33},{33,1},{2,34},{34,2},{3,35},{35,3},{4,36},{36... | collective-permute-start | bytes 405512 | tf_op jit(solution)/shard_map/ppermute | solution.py:35
  90.3 6.1 %collective-permute-done.24.other_ref = f32[264,128]{1,0:T(8,128)S(1)} collective-permute-done((f32[264,128]{1,0:T(8,128)S(1)}, f32[264,128]{1,0:T(8,128)S(1)}, u32[]{:S(2)}, u32[]{:S(2)}) %collective-permute-start.24) | collective-permute-done | bytes 135200 | tf_op jit(solution)/shard_map/ppermute | solution.py:35
  96.4 0.6 finish.1.p0_ref
  97.0 7.4 %collective-permute-start.26 = (f32[256,128]{1,0:T(8,128)S(1)}, f32[256,128]{1,0:T(8,128)S(1)}, u32[]{:S(2)}, u32[]{:S(2)}) collective-permute-start(f32[256,128]{1,0:T(8,128)S(1)} %finish.1.p0_ref), channel_id=1, source_target_pairs={{0,128},{64,192},{128,0},{192,64},{1,129},{65,193},{129,1},{193,65... | collective-permute-start | bytes 393224 | tf_op jit(solution)/shard_map/ppermute | solution.py:35
  104.5 1.2 %collective-permute-done.25.p1_ref = f32[256,128]{1,0:T(8,128)S(1)} collective-permute-done((f32[256,128]{1,0:T(8,128)S(1)}, f32[256,128]{1,0:T(8,128)S(1)}, u32[]{:S(2)}, u32[]{:S(2)}) %collective-permute-start.25) | collective-permute-done | bytes 131104 | tf_op jit(solution)/shard_map/ppermute | solution.py:35
  105.6 3.6 %collective-permute-done.26.p2_ref = f32[256,128]{1,0:T(8,128)S(1)} collective-permute-done((f32[256,128]{1,0:T(8,128)S(1)}, f32[256,128]{1,0:T(8,128)S(1)}, u32[]{:S(2)}, u32[]{:S(2)}) %collective-permute-start.26) | collective-permute-done | bytes 131104 | tf_op jit(solution)/shard_map/ppermute | solution.py:35
  109.3 0.7 collective-permute-done.27.p3_ref
  110.0 1.4 %place.1 = f32[1024,128]{1,0:T(8,128)} custom-call(s32[5]{0:T(128)S(1)} %stack.19.meta, f32[256,128]{1,0:T(8,128)S(1)} %finish.1.p0_ref, f32[256,128]{1,0:T(8,128)S(1)} %collective-permute-done.25.p1_ref, f32[256,128]{1,0:T(8,128)S(1)} %collective-permute-done.26.p2_ref, f32[256,128]{1,0:T(8,128)S(1)} %collective-permute-done.27.p3_ref), custom_call_target="tpu_custom_call" | custom-call | tf_op jit(solution)/shard_map/place/pallas_call | solution.py:224
  (49 shorter events, 1.8 us)
Async XLA Ops:
  1.9 6.6 %collective-permute-start = (bf16[144,128]{1,0:T(8,128)(2,1)S(1)}, bf16[144,128]{1,0:T(8,128)(2,1)S(1)}, u32[]{:S(2)}, u32[]{:S(2)}) collective-permute-start(bf16[144,128]{1,0:T(8,128)(2,1)S(1)} %get-tuple-element.13), channel_id=1, source_target_pairs={{0,2},{2,4},{4,6},{6,0},{1,3},{3,5},{5,7},{7,1},{8,10},{10,12},{12... | collective-permute-start | bytes 110600 | tf_op jit(solution)/shard_map/ppermute | solution.py:35
  4.4 4.5 %collective-permute-start.1 = (bf16[144,128]{1,0:T(8,128)(2,1)S(1)}, bf16[144,128]{1,0:T(8,128)(2,1)S(1)}, u32[]{:S(2)}, u32[]{:S(2)}) collective-permute-start(bf16[144,128]{1,0:T(8,128)(2,1)S(1)} %get-tuple-element.13), channel_id=1, source_target_pairs={{0,4},{2,6},{4,0},{6,2},{1,5},{3,7},{5,1},{7,3},{8,12},{10,14},{12... | collective-permute-start | bytes 110600 | tf_op jit(solution)/shard_map/ppermute | solution.py:35
  7.4 3.6 %collective-permute-start.2 = (bf16[144,128]{1,0:T(8,128)(2,1)S(1)}, bf16[144,128]{1,0:T(8,128)(2,1)S(1)}, u32[]{:S(2)}, u32[]{:S(2)}) collective-permute-start(bf16[144,128]{1,0:T(8,128)(2,1)S(1)} %get-tuple-element.13), channel_id=1, source_target_pairs={{0,6},{2,0},{4,2},{6,4},{1,7},{3,1},{5,3},{7,5},{8,14},{10,8},{12,... | collective-permute-start | bytes 110600 | tf_op jit(solution)/shard_map/ppermute | solution.py:35
  11.1 4.1 %collective-permute-start.3 = (bf16[576,128]{1,0:T(8,128)(2,1)S(1)}, bf16[576,128]{1,0:T(8,128)(2,1)S(1)}, u32[]{:S(2)}, u32[]{:S(2)}) collective-permute-start(bf16[576,128]{1,0:T(8,128)(2,1)S(1)} %get-tuple-element.59), channel_id=1, source_target_pairs={{0,8},{8,0},{16,24},{24,16},{1,9},{9,1},{17,25},{25,17},{2,10},{10... | collective-permute-start | bytes 442376 | tf_op jit(solution)/shard_map/ppermute | solution.py:35
  12.1 7.4 %collective-permute-start.4 = (bf16[576,128]{1,0:T(8,128)(2,1)S(1)}, bf16[576,128]{1,0:T(8,128)(2,1)S(1)}, u32[]{:S(2)}, u32[]{:S(2)}) collective-permute-start(bf16[576,128]{1,0:T(8,128)(2,1)S(1)} %get-tuple-element.59), channel_id=1, source_target_pairs={{0,16},{8,24},{16,0},{24,8},{1,17},{9,25},{17,1},{25,9},{2,18},{10... | collective-permute-start | bytes 442376 | tf_op jit(solution)/shard_map/ppermute | solution.py:35
  14.5 7.7 %collective-permute-start.5 = (bf16[576,128]{1,0:T(8,128)(2,1)S(1)}, bf16[576,128]{1,0:T(8,128)(2,1)S(1)}, u32[]{:S(2)}, u32[]{:S(2)}) collective-permute-start(bf16[576,128]{1,0:T(8,128)(2,1)S(1)} %get-tuple-element.59), channel_id=1, source_target_pairs={{0,24},{8,16},{16,8},{24,0},{1,25},{9,17},{17,9},{25,1},{2,26},{10... | collective-permute-start | bytes 442376 | tf_op jit(solution)/shard_map/ppermute | solution.py:35
  15.1 11.0 %copy-start.2 = (s32[48]{0:T(128)S(1)}, s32[48]{0:T(128)}, u32[]{:S(2)}) copy-start(s32[48]{0:T(128)} %rows.3) | copy-start | bytes 580
  15.1 11.0 %copy-start.3 = (s32[48]{0:T(128)S(1)}, s32[48]{0:T(128)}, u32[]{:S(2)}) copy-start(s32[48]{0:T(128)} %cols.3) | copy-start | bytes 580
  22.3 3.7 %collective-permute-start.6 = (bf16[2304,128]{1,0:T(8,128)(2,1)S(1)}, bf16[2304,128]{1,0:T(8,128)(2,1)S(1)}, u32[]{:S(2)}, u32[]{:S(2)}) collective-permute-start(bf16[2304,128]{1,0:T(8,128)(2,1)S(1)} %get-tuple-element.39), channel_id=1, source_target_pairs={{0,1},{1,0},{2,3},{3,2},{4,5},{5,4},{6,7},{7,6},{8,9},{9,8},{10,11... | collective-permute-start | bytes 1769480 | tf_op jit(solution)/shard_map/ppermute | solution.py:35
  26.1 46.6 %slice-start = ((s8[6291456]{0:T(1024)(128)(4,1)}), s8[4194304]{0:T(1024)(128)(4,1)S(1)}, s32[]{:S(2)}) async-start(s8[6291456]{0:T(1024)(128)(4,1)} %bitcast.4), calls=%async_computation | async-start | bytes 8388608
  30.2 5.0 %collective-permute-start.7 = (bf16[2048,128]{1,0:T(8,128)(2,1)S(1)}, bf16[2048,128]{1,0:T(8,128)(2,1)S(1)}, u32[]{:S(2)}, u32[]{:S(2)}) collective-permute-start(bf16[2048,128]{1,0:T(8,128)(2,1)S(1)} %get-tuple-element.16), channel_id=1, source_target_pairs={{0,1},{1,0},{2,3},{3,2},{4,5},{5,4},{6,7},{7,6},{8,9},{9,8},{10,11... | collective-permute-start | bytes 1572872 | tf_op jit(solution)/shard_map/ppermute | solution.py:35
  35.2 37.5 %slice-start.1 = ((s8[6291456]{0:T(1024)(128)(4,1)}), s8[2097152]{0:T(1024)(128)(4,1)S(1)}, s32[]{:S(2)}) async-start(s8[6291456]{0:T(1024)(128)(4,1)} %bitcast.4), calls=%async_computation.1 | async-start | bytes 4194304
  35.4 15.3 %copy-start.1 = (f32[128,128]{1,0:T(8,128)S(1)}, f32[128,128]{1,0:T(8,128)}, u32[]{:S(2)}) copy-start(f32[128,128]{1,0:T(8,128)} %cell_ref.3) | copy-start | bytes 196612
  35.4 8.5 %collective-permute-start.10 = (bf16[512,128]{1,0:T(8,128)(2,1)S(1)}, bf16[512,128]{1,0:T(8,128)(2,1)S(1)}, u32[]{:S(2)}, u32[]{:S(2)}) collective-permute-start(bf16[512,128]{1,0:T(8,128)(2,1)S(1)} %get-tuple-element.27), channel_id=1, source_target_pairs={{0,24},{8,16},{16,8},{24,0},{1,25},{9,17},{17,9},{25,1},{2,26},{10... | collective-permute-start | bytes 393224 | tf_op jit(solution)/shard_map/ppermute | solution.py:35
  36.4 7.5 %collective-permute-start.9 = (bf16[512,128]{1,0:T(8,128)(2,1)S(1)}, bf16[512,128]{1,0:T(8,128)(2,1)S(1)}, u32[]{:S(2)}, u32[]{:S(2)}) collective-permute-start(bf16[512,128]{1,0:T(8,128)(2,1)S(1)} %get-tuple-element.28), channel_id=1, source_target_pairs={{0,16},{8,24},{16,0},{24,8},{1,17},{9,25},{17,1},{25,9},{2,18},{10... | collective-permute-start | bytes 393224 | tf_op jit(solution)/shard_map/ppermute | solution.py:35
  36.4 8.2 %collective-permute-start.8 = (bf16[512,128]{1,0:T(8,128)(2,1)S(1)}, bf16[512,128]{1,0:T(8,128)(2,1)S(1)}, u32[]{:S(2)}, u32[]{:S(2)}) collective-permute-start(bf16[512,128]{1,0:T(8,128)(2,1)S(1)} %get-tuple-element.26), channel_id=1, source_target_pairs={{0,8},{8,0},{16,24},{24,16},{1,9},{9,1},{17,25},{25,17},{2,10},{10... | collective-permute-start | bytes 393224 | tf_op jit(solution)/shard_map/ppermute | solution.py:35
  44.7 5.0 %collective-permute-start.11 = (f32[128,128]{1,0:T(8,128)S(1)}, f32[128,128]{1,0:T(8,128)S(1)}, u32[]{:S(2)}, u32[]{:S(2)}) collective-permute-start(f32[128,128]{1,0:T(8,128)S(1)} %get-tuple-element.31), channel_id=1, source_target_pairs={{0,2},{2,4},{4,6},{6,0},{1,3},{3,5},{5,7},{7,1},{8,10},{10,12},{12... | collective-permute-start | bytes 196616 | tf_op jit(solution)/shard_map/ppermute | solution.py:35
  44.8 4.9 %collective-permute-start.12 = (f32[128,128]{1,0:T(8,128)S(1)}, f32[128,128]{1,0:T(8,128)S(1)}, u32[]{:S(2)}, u32[]{:S(2)}) collective-permute-start(f32[128,128]{1,0:T(8,128)S(1)} %get-tuple-element.30), channel_id=1, source_target_pairs={{0,4},{2,6},{4,0},{6,2},{1,5},{3,7},{5,1},{7,3},{8,12},{10,14},{12... | collective-permute-start | bytes 196616 | tf_op jit(solution)/shard_map/ppermute | solution.py:35
  45.3 5.4 %collective-permute-start.13 = (f32[128,128]{1,0:T(8,128)S(1)}, f32[128,128]{1,0:T(8,128)S(1)}, u32[]{:S(2)}, u32[]{:S(2)}) collective-permute-start(f32[128,128]{1,0:T(8,128)S(1)} %get-tuple-element.29), channel_id=1, source_target_pairs={{0,6},{2,0},{4,2},{6,4},{1,7},{3,1},{5,3},{7,5},{8,14},{10,8},{12,... | collective-permute-start | bytes 196616 | tf_op jit(solution)/shard_map/ppermute | solution.py:35
  51.4 5.5 %collective-permute-start.14 = (bf16[144,128]{1,0:T(8,128)(2,1)S(1)}, bf16[144,128]{1,0:T(8,128)(2,1)S(1)}, u32[]{:S(2)}, u32[]{:S(2)}) collective-permute-start(bf16[144,128]{1,0:T(8,128)(2,1)S(1)} %get-tuple-element.19), channel_id=1, source_target_pairs={{0,2},{2,4},{4,6},{6,0},{1,3},{3,5},{5,7},{7,1},{8,10},{10,12},{12... | collective-permute-start | bytes 110600 | tf_op jit(solution)/shard_map/ppermute | solution.py:35
  54.5 4.1 %collective-permute-start.15 = (bf16[144,128]{1,0:T(8,128)(2,1)S(1)}, bf16[144,128]{1,0:T(8,128)(2,1)S(1)}, u32[]{:S(2)}, u32[]{:S(2)}) collective-permute-start(bf16[144,128]{1,0:T(8,128)(2,1)S(1)} %get-tuple-element.19), channel_id=1, source_target_pairs={{0,4},{2,6},{4,0},{6,2},{1,5},{3,7},{5,1},{7,3},{8,12},{10,14},{12... | collective-permute-start | bytes 110600 | tf_op jit(solution)/shard_map/ppermute | solution.py:35
  54.8 3.8 %collective-permute-start.16 = (bf16[144,128]{1,0:T(8,128)(2,1)S(1)}, bf16[144,128]{1,0:T(8,128)(2,1)S(1)}, u32[]{:S(2)}, u32[]{:S(2)}) collective-permute-start(bf16[144,128]{1,0:T(8,128)(2,1)S(1)} %get-tuple-element.19), channel_id=1, source_target_pairs={{0,6},{2,0},{4,2},{6,4},{1,7},{3,1},{5,3},{7,5},{8,14},{10,8},{12,... | collective-permute-start | bytes 110600 | tf_op jit(solution)/shard_map/ppermute | solution.py:35
  58.6 4.1 %collective-permute-start.17 = (bf16[576,128]{1,0:T(8,128)(2,1)S(1)}, bf16[576,128]{1,0:T(8,128)(2,1)S(1)}, u32[]{:S(2)}, u32[]{:S(2)}) collective-permute-start(bf16[576,128]{1,0:T(8,128)(2,1)S(1)} %get-tuple-element.47), channel_id=1, source_target_pairs={{0,8},{8,0},{16,24},{24,16},{1,9},{9,1},{17,25},{25,17},{2,10},{10... | collective-permute-start | bytes 442376 | tf_op jit(solution)/shard_map/ppermute | solution.py:35
  58.7 6.2 %collective-permute-start.18 = (bf16[576,128]{1,0:T(8,128)(2,1)S(1)}, bf16[576,128]{1,0:T(8,128)(2,1)S(1)}, u32[]{:S(2)}, u32[]{:S(2)}) collective-permute-start(bf16[576,128]{1,0:T(8,128)(2,1)S(1)} %get-tuple-element.47), channel_id=1, source_target_pairs={{0,16},{8,24},{16,0},{24,8},{1,17},{9,25},{17,1},{25,9},{2,18},{10... | collective-permute-start | bytes 442376 | tf_op jit(solution)/shard_map/ppermute | solution.py:35
  60.8 5.7 %collective-permute-start.19 = (bf16[576,128]{1,0:T(8,128)(2,1)S(1)}, bf16[576,128]{1,0:T(8,128)(2,1)S(1)}, u32[]{:S(2)}, u32[]{:S(2)}) collective-permute-start(bf16[576,128]{1,0:T(8,128)(2,1)S(1)} %get-tuple-element.47), channel_id=1, source_target_pairs={{0,24},{8,16},{16,8},{24,0},{1,25},{9,17},{17,9},{25,1},{2,26},{10... | collective-permute-start | bytes 442376 | tf_op jit(solution)/shard_map/ppermute | solution.py:35
  66.6 6.0 %collective-permute-start.20 = (bf16[2304,128]{1,0:T(8,128)(2,1)S(1)}, bf16[2304,128]{1,0:T(8,128)(2,1)S(1)}, u32[]{:S(2)}, u32[]{:S(2)}) collective-permute-start(bf16[2304,128]{1,0:T(8,128)(2,1)S(1)} %get-tuple-element.33), channel_id=1, source_target_pairs={{0,1},{1,0},{2,3},{3,2},{4,5},{5,4},{6,7},{7,6},{8,9},{9,8},{10,11... | collective-permute-start | bytes 1769480 | tf_op jit(solution)/shard_map/ppermute | solution.py:35
  72.7 23.7 %copy-start = (f32[1024,128]{1,0:T(8,128)S(1)}, f32[1024,128]{1,0:T(8,128)}, u32[]{:S(2)}) copy-start(f32[1024,128]{1,0:T(8,128)} %gene_ref.3) | copy-start | bytes 1572868
  75.1 9.2 %collective-permute-start.21 = (f32[264,128]{1,0:T(8,128)S(1)}, f32[264,128]{1,0:T(8,128)S(1)}, u32[]{:S(2)}, u32[]{:S(2)}) collective-permute-start(f32[264,128]{1,0:T(8,128)S(1)} %get-tuple-element.21), channel_id=1, source_target_pairs={{0,64},{64,128},{128,192},{192,0},{1,65},{65,129},{129,193},{193,1... | collective-permute-start | bytes 405512 | tf_op jit(solution)/shard_map/ppermute | solution.py:35
  75.2 12.4 %collective-permute-start.22 = (f32[264,128]{1,0:T(8,128)S(1)}, f32[264,128]{1,0:T(8,128)S(1)}, u32[]{:S(2)}, u32[]{:S(2)}) collective-permute-start(f32[264,128]{1,0:T(8,128)S(1)} %get-tuple-element.22), channel_id=1, source_target_pairs={{0,128},{64,192},{128,0},{192,64},{1,129},{65,193},{129,1},{193,65... | collective-permute-start | bytes 405512 | tf_op jit(solution)/shard_map/ppermute | solution.py:35
  82.2 5.6 %collective-permute-start.23 = (f32[264,128]{1,0:T(8,128)S(1)}, f32[264,128]{1,0:T(8,128)S(1)}, u32[]{:S(2)}, u32[]{:S(2)}) collective-permute-start(f32[264,128]{1,0:T(8,128)S(1)} %get-tuple-element.23), channel_id=1, source_target_pairs={{0,192},{64,0},{128,64},{192,128},{1,193},{65,1},{129,65},{193,129... | collective-permute-start | bytes 405512 | tf_op jit(solution)/shard_map/ppermute | solution.py:35
  87.8 8.6 %collective-permute-start.24 = (f32[264,128]{1,0:T(8,128)S(1)}, f32[264,128]{1,0:T(8,128)S(1)}, u32[]{:S(2)}, u32[]{:S(2)}) collective-permute-start(f32[264,128]{1,0:T(8,128)S(1)} %fold.1.mine_ref), channel_id=1, source_target_pairs={{0,32},{32,0},{1,33},{33,1},{2,34},{34,2},{3,35},{35,3},{4,36},{36... | collective-permute-start | bytes 405512 | tf_op jit(solution)/shard_map/ppermute | solution.py:35
  97.0 8.7 %collective-permute-start.25 = (f32[256,128]{1,0:T(8,128)S(1)}, f32[256,128]{1,0:T(8,128)S(1)}, u32[]{:S(2)}, u32[]{:S(2)}) collective-permute-start(f32[256,128]{1,0:T(8,128)S(1)} %finish.1.p0_ref), channel_id=1, source_target_pairs={{0,64},{64,128},{128,192},{192,0},{1,65},{65,129},{129,193},{193,1... | collective-permute-start | bytes 393224 | tf_op jit(solution)/shard_map/ppermute | solution.py:35
  97.0 12.2 %collective-permute-start.26 = (f32[256,128]{1,0:T(8,128)S(1)}, f32[256,128]{1,0:T(8,128)S(1)}, u32[]{:S(2)}, u32[]{:S(2)}) collective-permute-start(f32[256,128]{1,0:T(8,128)S(1)} %finish.1.p0_ref), channel_id=1, source_target_pairs={{0,128},{64,192},{128,0},{192,64},{1,129},{65,193},{129,1},{193,65... | collective-permute-start | bytes 393224 | tf_op jit(solution)/shard_map/ppermute | solution.py:35
  104.5 5.5 %collective-permute-start.27 = (f32[256,128]{1,0:T(8,128)S(1)}, f32[256,128]{1,0:T(8,128)S(1)}, u32[]{:S(2)}, u32[]{:S(2)}) collective-permute-start(f32[256,128]{1,0:T(8,128)S(1)} %finish.1.p0_ref), channel_id=1, source_target_pairs={{0,192},{64,0},{128,64},{192,128},{1,193},{65,1},{129,65},{193,129... | collective-permute-start | bytes 393224 | tf_op jit(solution)/shard_map/ppermute | solution.py:35

commit v3 on v2

--- a/solution.py
+++ b/solution.py
@@ -27,7 +27,13 @@
 
 
 def partner(axis, i, step):
+    if axis == "zl":
+        return label((label(i) + step) % 4)
     return i + step if axis in SHIFTED else i ^ step
+
+
+def label(i):
+    return i ^ (i >> 1)
 
 
 def swap(value, axis, step):
@@ -77,13 +83,13 @@
 
 def slot_base(meta, row, other):
     dx = meta[0] ^ (row >> 2)
-    dz = (meta[1] - (row & 3)) & 3
+    dz = (label(meta[1]) - label(row & 3)) & 3
     return pl.multiple_of((other * 16 + dx * 4 + dz) * PAD, 16)
 
 
 def unit_base(meta, row):
     dx = meta[0] ^ (row >> 2)
-    dz = ((row & 3) - meta[1]) & 3
+    dz = (label(row & 3) - label(meta[1])) & 3
     return pl.multiple_of((dx * 4 + dz) * HALF, HALF)
 
 
@@ -153,8 +159,23 @@
 
 
 def genes_kernel(
-    meta, rows, cols, blocks_ref, g_ref, hb_ref, own_ref, s1_ref, s2_ref, s3_ref, acc
+    meta,
+    rows,
+    cols,
+    blocks_ref,
+    g_ref,
+    hb_ref,
+    new_ref,
+    own_ref,
+    s1_ref,
+    s2_ref,
+    s3_ref,
+    out_ref,
+    acc,
+    sem,
 ):
+    leaving = pltpu.make_async_copy(new_ref, out_ref, sem)
+    leaving.start()
     acc[...] = jnp.zeros_like(acc)
     total = group_sum(g_ref)
     count = meta[3]
@@ -187,25 +208,20 @@
     for k, ref in enumerate((own_ref, s1_ref, s2_ref, s3_ref)):
         ref[:BLK, :] = acc[k]
         ref[BLK:, :] = total
+    leaving.wait()
 
 
 def fold_kernel(own_ref, r1_ref, r2_ref, r3_ref, out_ref):
     out_ref[...] = own_ref[...] + r1_ref[...] + r2_ref[...] + r3_ref[...]
 
 
-def finish_kernel(meta, mine_ref, other_ref, gene_ref, out_ref):
-    both = mine_ref[...] + other_ref[...]
-    at = pl.ds(pl.multiple_of(meta[4] * BLK, BLK), BLK)
-    out_ref[...] = gene_ref[at, :] * both[:BLK] / both[BLK : BLK + 1]
-
-
-def place_kernel(meta, p0_ref, p1_ref, p2_ref, p3_ref, out_ref, sems):
+def place_kernel(meta, gene_ref, p0_ref, p1_ref, p2_ref, p3_ref, out_ref, fresh, sems):
     copies = []
     for k, ref in enumerate((p0_ref, p1_ref, p2_ref, p3_ref)):
         at = pl.ds(pl.multiple_of(((meta[4] - k) & 3) * BLK, BLK), BLK)
-        copies.append(pltpu.make_async_copy(ref, out_ref.at[at, :], sems.at[k]))
-    for copy in copies:
-        copy.start()
+        fresh[k] = gene_ref[at, :] * ref[:BLK, :] / ref[BLK : BLK + 1, :]
+        copies.append(pltpu.make_async_copy(fresh.at[k], out_ref.at[at, :], sems.at[k]))
+        copies[k].start()
     for copy in copies:
         copy.wait()
 
@@ -285,7 +301,7 @@
         part = part + arrived.astype(F32)
     own = part[:HALF]
     sent = [swap(part[k * HALF : (k + 1) * HALF], "zl", k) for k in (1, 2, 3)]
-    cell_new, pay = call(
+    fresh, pay = call(
         update_kernel,
         (shape((HALF, R), F32), shape((PAD, R), BF)),
         (own, *sent, cell_factor, gene_sums),
@@ -293,32 +309,26 @@
         name="update",
     )
     g2 = gathered(pay)
-    mine, *send = call(
+    mine, *send, cell_new = call(
         genes_kernel,
-        (shape((BLK + 8, R), F32),) * 4,
-        (meta, block_rows, block_cols, blocks, g2, hb),
-        "sssvvv",
-        scratch=[pltpu.VMEM((4, BLK, R), F32)],
+        (shape((BLK + 8, R), F32),) * 4 + (shape((HALF, R), F32),),
+        (meta, block_rows, block_cols, blocks, g2, hb, fresh),
+        "sssvvvv",
+        gives="vvvva",
+        scratch=[pltpu.VMEM((4, BLK, R), F32), pltpu.SemaphoreType.DMA],
         name="genes",
     )
     arrived = [swap(send[k - 1], "y", k) for k in (1, 2, 3)]
     folded = call(fold_kernel, shape((BLK + 8, R), F32), (mine, *arrived), "vvvv", name="fold")
-    other = swap(folded, "zh", 1)
-    fresh = call(
-        finish_kernel,
-        shape((BLK, R), F32),
-        (meta, folded, other, gene_factor),
-        "svvv",
-        name="finish",
-    )
-    parts = [fresh] + [swap(fresh, "y", k) for k in (1, 2, 3)]
+    both = folded + swap(folded, "zh", 1)
+    parts = [both] + [swap(both, "y", k) for k in (1, 2, 3)]
     gene_new = call(
         place_kernel,
         shape((genes, R), F32),
-        (meta, *parts),
-        "svvvv",
+        (meta, gene_factor, *parts),
+        "svvvvv",
         gives="a",
-        scratch=[pltpu.SemaphoreType.DMA((4,))],
+        scratch=[pltpu.VMEM((4, BLK, R), F32), pltpu.SemaphoreType.DMA((4,))],
         name="place",
     )
     return (cell_new, gene_new)

time: 111 us -> 110 us (level)
  Pallas kernels: 10.3 us -> 9.16 us
    pallas_call x7 -> x6, Pallas kernels: 10.3 us -> 9.16 us  [call(): pl.pallas_call(kernel, out_shape=outs, in_specs=[spec[kind]() for kind in...]
  transfers between devices with their start and end apart: 28 -> 28, of which waited for: 24 -> 26; matrix products, arithmetic and copies ran while one was open for 0% -> 0% of each run, Pallas kernels for 0% -> 0%
where the time goes in v3:
time: 110 us
  starting transfers between devices  53.3 us (48%)
  waiting for transfers between devices  44.5 us (40%)
  Pallas kernels  9.16 us (8%)
  between operations  1.68 us (2%)
    ppermute x28, starting transfers between devices, swap(): lax.ppermute(value, axis, [(i, partner(axis, i, step) % count) for i in r...  53.3 us
    ppermute x28, waiting for transfers between devices, swap(): lax.ppermute(value, axis, [(i, partner(axis, i, step) % count) for i in r...  44.5 us
    pallas_call x6, Pallas kernels, call(): pl.pallas_call(kernel, out_shape=outs, in_specs=[spec[kind]() for kind in...  9.16 us
  transfers between devices with their start and end apart: 28, of which 26 were waited for; matrix products, arithmetic and copies ran while one was open for 0% of the time, Pallas kernels for 0%

profile of v3, /device:TPU:1, one launch (start us, length us, event | category | flops | bytes accessed | tf_op | source)
XLA Modules:
  0.0 109.6 jit_solution(16431098544164209346)
XLA Ops:
  0.6 1.2 %prep.1 = (bf16[144,128]{1,0:T(8,128)(2,1)S(1)}, bf16[1024,128]{1,0:T(8,128)(2,1)S(1)}) custom-call(f32[128,128]{1,0:T(8,128)} %cell_ref.3, f32[1024,128]{1,0:T(8,128)} %gene_ref.3), custom_call_target="tpu_custom_call" | custom-call | tf_op jit(solution)/shard_map/prep/pallas_call | solution.py:240
  1.9 2.5 %collective-permute-start = (bf16[144,128]{1,0:T(8,128)(2,1)S(1)}, bf16[144,128]{1,0:T(8,128)(2,1)S(1)}, u32[]{:S(2)}, u32[]{:S(2)}) collective-permute-start(bf16[144,128]{1,0:T(8,128)(2,1)S(1)} %get-tuple-element.14), channel_id=1, source_target_pairs={{0,2},{2,6},{4,0},{6,4},{1,3},{3,7},{5,1},{7,5},{8,10},{10,14},{12... | collective-permute-start | bytes 110600 | tf_op jit(solution)/shard_map/ppermute | solution.py:41
  4.4 2.8 %collective-permute-start.1 = (bf16[144,128]{1,0:T(8,128)(2,1)S(1)}, bf16[144,128]{1,0:T(8,128)(2,1)S(1)}, u32[]{:S(2)}, u32[]{:S(2)}) collective-permute-start(bf16[144,128]{1,0:T(8,128)(2,1)S(1)} %get-tuple-element.14), channel_id=1, source_target_pairs={{0,6},{2,4},{4,2},{6,0},{1,7},{3,5},{5,3},{7,1},{8,14},{10,12},{12... | collective-permute-start | bytes 110600 | tf_op jit(solution)/shard_map/ppermute | solution.py:41
  7.2 1.4 %collective-permute-start.2 = (bf16[144,128]{1,0:T(8,128)(2,1)S(1)}, bf16[144,128]{1,0:T(8,128)(2,1)S(1)}, u32[]{:S(2)}, u32[]{:S(2)}) collective-permute-start(bf16[144,128]{1,0:T(8,128)(2,1)S(1)} %get-tuple-element.14), channel_id=1, source_target_pairs={{0,4},{2,0},{4,6},{6,2},{1,5},{3,1},{5,7},{7,3},{8,12},{10,8},{12,... | collective-permute-start | bytes 110600 | tf_op jit(solution)/shard_map/ppermute | solution.py:41
  9.0 1.3 %collective-permute-done.2 = bf16[144,128]{1,0:T(8,128)(2,1)S(1)} collective-permute-done((bf16[144,128]{1,0:T(8,128)(2,1)S(1)}, bf16[144,128]{1,0:T(8,128)(2,1)S(1)}, u32[]{:S(2)}, u32[]{:S(2)}) %collective-permute-start.2) | collective-permute-done | bytes 36896 | tf_op jit(solution)/shard_map/ppermute | solution.py:41
  10.3 1.3 %collective-permute-start.3 = (bf16[576,128]{1,0:T(8,128)(2,1)S(1)}, bf16[576,128]{1,0:T(8,128)(2,1)S(1)}, u32[]{:S(2)}, u32[]{:S(2)}) collective-permute-start(bf16[576,128]{1,0:T(8,128)(2,1)S(1)} %get-tuple-element.61), channel_id=1, source_target_pairs={{0,8},{8,0},{16,24},{24,16},{1,9},{9,1},{17,25},{25,17},{2,10},{10... | collective-permute-start | bytes 442376 | tf_op jit(solution)/shard_map/ppermute | solution.py:41
  11.6 2.5 %collective-permute-start.4 = (bf16[576,128]{1,0:T(8,128)(2,1)S(1)}, bf16[576,128]{1,0:T(8,128)(2,1)S(1)}, u32[]{:S(2)}, u32[]{:S(2)}) collective-permute-start(bf16[576,128]{1,0:T(8,128)(2,1)S(1)} %get-tuple-element.61), channel_id=1, source_target_pairs={{0,16},{8,24},{16,0},{24,8},{1,17},{9,25},{17,1},{25,9},{2,18},{10... | collective-permute-start | bytes 442376 | tf_op jit(solution)/shard_map/ppermute | solution.py:41
  14.5 4.5 %collective-permute-done.4 = bf16[576,128]{1,0:T(8,128)(2,1)S(1)} collective-permute-done((bf16[576,128]{1,0:T(8,128)(2,1)S(1)}, bf16[576,128]{1,0:T(8,128)(2,1)S(1)}, u32[]{:S(2)}, u32[]{:S(2)}) %collective-permute-start.4) | collective-permute-done | bytes 147488 | tf_op jit(solution)/shard_map/ppermute | solution.py:41
  19.0 2.6 %collective-permute-done.5 = bf16[576,128]{1,0:T(8,128)(2,1)S(1)} collective-permute-done((bf16[576,128]{1,0:T(8,128)(2,1)S(1)}, bf16[576,128]{1,0:T(8,128)(2,1)S(1)}, u32[]{:S(2)}, u32[]{:S(2)}) %collective-permute-start.5) | collective-permute-done | bytes 147488 | tf_op jit(solution)/shard_map/ppermute | solution.py:41
  21.7 2.2 %collective-permute-start.6 = (bf16[2304,128]{1,0:T(8,128)(2,1)S(1)}, bf16[2304,128]{1,0:T(8,128)(2,1)S(1)}, u32[]{:S(2)}, u32[]{:S(2)}) collective-permute-start(bf16[2304,128]{1,0:T(8,128)(2,1)S(1)} %get-tuple-element.41), channel_id=1, source_target_pairs={{0,1},{1,0},{2,3},{3,2},{4,5},{5,4},{6,7},{7,6},{8,9},{9,8},{10,11... | collective-permute-start | bytes 1769480 | tf_op jit(solution)/shard_map/ppermute | solution.py:41
  24.7 0.9 collective-permute-done.6
  25.7 4.1 %cells.1 = (f32[2048,128]{1,0:T(8,128)S(1)}, bf16[2048,128]{1,0:T(8,128)(2,1)S(1)}, f32[8,128]{1,0:T(8,128)S(1)}) custom-call(s32[5]{0:T(128)S(1)} %stack.19.meta, s32[48]{0:T(128)S(1)} %copy-done.2, s32[48]{0:T(128)S(1)} %copy-done.3, bf16[48,256,256]{2,1,0:T(8,128)(2,1)} %blocks_ref.3, bf16[4608,128]{1,0:T(8,128)(2,1)S(1)} %constant_dynamic-update-slice_fusion.11.g_ref, ...), custom_call_target="tpu_custom_call" | custom-call | tf_op jit(solution)/shard_map/cells/pallas_call | solution.py:240
  29.8 2.0 %collective-permute-start.7 = (bf16[2048,128]{1,0:T(8,128)(2,1)S(1)}, bf16[2048,128]{1,0:T(8,128)(2,1)S(1)}, u32[]{:S(2)}, u32[]{:S(2)}) collective-permute-start(bf16[2048,128]{1,0:T(8,128)(2,1)S(1)} %get-tuple-element.17), channel_id=1, source_target_pairs={{0,1},{1,0},{2,3},{3,2},{4,5},{5,4},{6,7},{7,6},{8,9},{9,8},{10,11... | collective-permute-start | bytes 1572872 | tf_op jit(solution)/shard_map/ppermute | solution.py:41
  31.7 1.5 %collective-permute-done.7 = bf16[2048,128]{1,0:T(8,128)(2,1)S(1)} collective-permute-done((bf16[2048,128]{1,0:T(8,128)(2,1)S(1)}, bf16[2048,128]{1,0:T(8,128)(2,1)S(1)}, u32[]{:S(2)}, u32[]{:S(2)}) %collective-permute-start.7) | collective-permute-done | bytes 524320 | tf_op jit(solution)/shard_map/ppermute | solution.py:41
  33.6 3.7 %collective-permute-start.9 = (bf16[512,128]{1,0:T(8,128)(2,1)S(1)}, bf16[512,128]{1,0:T(8,128)(2,1)S(1)}, u32[]{:S(2)}, u32[]{:S(2)}) collective-permute-start(bf16[512,128]{1,0:T(8,128)(2,1)S(1)} %get-tuple-element.30), channel_id=1, source_target_pairs={{0,16},{8,24},{16,0},{24,8},{1,17},{9,25},{17,1},{25,9},{2,18},{10... | collective-permute-start | bytes 393224 | tf_op jit(solution)/shard_map/ppermute | solution.py:41
  37.4 2.1 %collective-permute-done.10 = bf16[512,128]{1,0:T(8,128)(2,1)S(1)} collective-permute-done((bf16[512,128]{1,0:T(8,128)(2,1)S(1)}, bf16[512,128]{1,0:T(8,128)(2,1)S(1)}, u32[]{:S(2)}, u32[]{:S(2)}) %collective-permute-start.10) | collective-permute-done | bytes 131104 | tf_op jit(solution)/shard_map/ppermute | solution.py:41
  39.5 3.7 %collective-permute-done.9 = bf16[512,128]{1,0:T(8,128)(2,1)S(1)} collective-permute-done((bf16[512,128]{1,0:T(8,128)(2,1)S(1)}, bf16[512,128]{1,0:T(8,128)(2,1)S(1)}, u32[]{:S(2)}, u32[]{:S(2)}) %collective-permute-start.9) | collective-permute-done | bytes 131104 | tf_op jit(solution)/shard_map/ppermute | solution.py:41
  43.2 0.8 collective-permute-start.11
  44.0 2.7 %collective-permute-start.12 = (f32[128,128]{1,0:T(8,128)S(1)}, f32[128,128]{1,0:T(8,128)S(1)}, u32[]{:S(2)}, u32[]{:S(2)}) collective-permute-start(f32[128,128]{1,0:T(8,128)S(1)} %get-tuple-element.32), channel_id=1, source_target_pairs={{0,6},{2,4},{4,2},{6,0},{1,7},{3,5},{5,3},{7,1},{8,14},{10,12},{12... | collective-permute-start | bytes 196616 | tf_op jit(solution)/shard_map/ppermute | solution.py:41
  46.7 0.6 collective-permute-done.11.r1_ref
  47.3 1.8 %collective-permute-done.12.r2_ref = f32[128,128]{1,0:T(8,128)S(1)} collective-permute-done((f32[128,128]{1,0:T(8,128)S(1)}, f32[128,128]{1,0:T(8,128)S(1)}, u32[]{:S(2)}, u32[]{:S(2)}) %collective-permute-start.12) | collective-permute-done | bytes 65568 | tf_op jit(solution)/shard_map/ppermute | solution.py:41
  49.1 1.3 %collective-permute-done.13.r3_ref = f32[128,128]{1,0:T(8,128)S(1)} collective-permute-done((f32[128,128]{1,0:T(8,128)S(1)}, f32[128,128]{1,0:T(8,128)S(1)}, u32[]{:S(2)}, u32[]{:S(2)}) %collective-permute-start.13) | collective-permute-done | bytes 65568 | tf_op jit(solution)/shard_map/ppermute | solution.py:41
  50.6 2.6 %collective-permute-start.15 = (bf16[144,128]{1,0:T(8,128)(2,1)S(1)}, bf16[144,128]{1,0:T(8,128)(2,1)S(1)}, u32[]{:S(2)}, u32[]{:S(2)}) collective-permute-start(bf16[144,128]{1,0:T(8,128)(2,1)S(1)} %get-tuple-element.19), channel_id=1, source_target_pairs={{0,6},{2,4},{4,2},{6,0},{1,7},{3,5},{5,3},{7,1},{8,14},{10,12},{12... | collective-permute-start | bytes 110600 | tf_op jit(solution)/shard_map/ppermute | solution.py:41
  53.1 0.5 collective-permute-start.16
  53.7 0.6 collective-permute-done.14
  54.3 1.2 %collective-permute-done.15 = bf16[144,128]{1,0:T(8,128)(2,1)S(1)} collective-permute-done((bf16[144,128]{1,0:T(8,128)(2,1)S(1)}, bf16[144,128]{1,0:T(8,128)(2,1)S(1)}, u32[]{:S(2)}, u32[]{:S(2)}) %collective-permute-start.15) | collective-permute-done | bytes 36896 | tf_op jit(solution)/shard_map/ppermute | solution.py:41
  55.5 0.5 collective-permute-done.16
  56.1 2.5 %collective-permute-start.18 = (bf16[576,128]{1,0:T(8,128)(2,1)S(1)}, bf16[576,128]{1,0:T(8,128)(2,1)S(1)}, u32[]{:S(2)}, u32[]{:S(2)}) collective-permute-start(bf16[576,128]{1,0:T(8,128)(2,1)S(1)} %get-tuple-element.49), channel_id=1, source_target_pairs={{0,16},{8,24},{16,0},{24,8},{1,17},{9,25},{17,1},{25,9},{2,18},{10... | collective-permute-start | bytes 442376 | tf_op jit(solution)/shard_map/ppermute | solution.py:41
  58.6 1.3 %collective-permute-start.19 = (bf16[576,128]{1,0:T(8,128)(2,1)S(1)}, bf16[576,128]{1,0:T(8,128)(2,1)S(1)}, u32[]{:S(2)}, u32[]{:S(2)}) collective-permute-start(bf16[576,128]{1,0:T(8,128)(2,1)S(1)} %get-tuple-element.49), channel_id=1, source_target_pairs={{0,24},{8,16},{16,8},{24,0},{1,25},{9,17},{17,9},{25,1},{2,26},{10... | collective-permute-start | bytes 442376 | tf_op jit(solution)/shard_map/ppermute | solution.py:41
  60.1 2.6 %collective-permute-done.18 = bf16[576,128]{1,0:T(8,128)(2,1)S(1)} collective-permute-done((bf16[576,128]{1,0:T(8,128)(2,1)S(1)}, bf16[576,128]{1,0:T(8,128)(2,1)S(1)}, u32[]{:S(2)}, u32[]{:S(2)}) %collective-permute-start.18) | collective-permute-done | bytes 147488 | tf_op jit(solution)/shard_map/ppermute | solution.py:41
  62.8 1.5 %collective-permute-done.19 = bf16[576,128]{1,0:T(8,128)(2,1)S(1)} collective-permute-done((bf16[576,128]{1,0:T(8,128)(2,1)S(1)}, bf16[576,128]{1,0:T(8,128)(2,1)S(1)}, u32[]{:S(2)}, u32[]{:S(2)}) %collective-permute-start.19) | collective-permute-done | bytes 147488 | tf_op jit(solution)/shard_map/ppermute | solution.py:41
  64.3 5.6 %collective-permute-start.20 = (bf16[2304,128]{1,0:T(8,128)(2,1)S(1)}, bf16[2304,128]{1,0:T(8,128)(2,1)S(1)}, u32[]{:S(2)}, u32[]{:S(2)}) collective-permute-start(bf16[2304,128]{1,0:T(8,128)(2,1)S(1)} %get-tuple-element.35), channel_id=1, source_target_pairs={{0,1},{1,0},{2,3},{3,2},{4,5},{5,4},{6,7},{7,6},{8,9},{9,8},{10,11... | collective-permute-start | bytes 1769480 | tf_op jit(solution)/shard_map/ppermute | solution.py:41
  69.9 1.6 %collective-permute-done.20 = bf16[2304,128]{1,0:T(8,128)(2,1)S(1)} collective-permute-done((bf16[2304,128]{1,0:T(8,128)(2,1)S(1)}, bf16[2304,128]{1,0:T(8,128)(2,1)S(1)}, u32[]{:S(2)}, u32[]{:S(2)}) %collective-permute-start.20) | collective-permute-done | bytes 589856 | tf_op jit(solution)/shard_map/ppermute | solution.py:41
  71.7 2.4 %genes.1 = (f32[264,128]{1,0:T(8,128)S(1)}, f32[264,128]{1,0:T(8,128)S(1)}, f32[264,128]{1,0:T(8,128)S(1)}, f32[264,128]{1,0:T(8,128)S(1)}, f32[128,128]{1,0:T(8,128)}) custom-call(s32[5]{0:T(128)S(1)} %stack.19.meta, s32[48]{0:T(128)S(1)} %copy-done.2, s32[48]{0:T(128)S(1)} %copy-done.3, bf16[48,256,256]{2,1,0:T(8,128)(2,1)S(1)} %bitcast.5, ...), custom_call_target="tpu_custom_call" | custom-call | tf_op jit(solution)/shard_map/genes/pallas_call | solution.py:240
  74.1 5.8 %collective-permute-start.21 = (f32[264,128]{1,0:T(8,128)S(1)}, f32[264,128]{1,0:T(8,128)S(1)}, u32[]{:S(2)}, u32[]{:S(2)}) collective-permute-start(f32[264,128]{1,0:T(8,128)S(1)} %get-tuple-element.23), channel_id=1, source_target_pairs={{0,64},{64,128},{128,192},{192,0},{1,65},{65,129},{129,193},{193,1... | collective-permute-start | bytes 405512 | tf_op jit(solution)/shard_map/ppermute | solution.py:41
  79.9 2.5 %collective-permute-start.23 = (f32[264,128]{1,0:T(8,128)S(1)}, f32[264,128]{1,0:T(8,128)S(1)}, u32[]{:S(2)}, u32[]{:S(2)}) collective-permute-start(f32[264,128]{1,0:T(8,128)S(1)} %get-tuple-element.25), channel_id=1, source_target_pairs={{0,192},{64,0},{128,64},{192,128},{1,193},{65,1},{129,65},{193,129... | collective-permute-start | bytes 405512 | tf_op jit(solution)/shard_map/ppermute | solution.py:41
  82.4 0.6 collective-permute-done.21.r1_ref
  83.0 2.8 %collective-permute-done.22.r2_ref = f32[264,128]{1,0:T(8,128)S(1)} collective-permute-done((f32[264,128]{1,0:T(8,128)S(1)}, f32[264,128]{1,0:T(8,128)S(1)}, u32[]{:S(2)}, u32[]{:S(2)}) %collective-permute-start.22) | collective-permute-done | bytes 135200 | tf_op jit(solution)/shard_map/ppermute | solution.py:41
  85.8 1.0 collective-permute-done.23.r3_ref
  86.8 5.5 %collective-permute-start.24 = (f32[264,128]{1,0:T(8,128)S(1)}, f32[264,128]{1,0:T(8,128)S(1)}, u32[]{:S(2)}, u32[]{:S(2)}) collective-permute-start(f32[264,128]{1,0:T(8,128)S(1)} %fold.1), channel_id=1, source_target_pairs={{0,32},{32,0},{1,33},{33,1},{2,34},{34,2},{3,35},{35,3},{4,36},{36... | collective-permute-start | bytes 405512 | tf_op jit(solution)/shard_map/ppermute | solution.py:41
  92.3 6.0 %collective-permute-done.24 = f32[264,128]{1,0:T(8,128)S(1)} collective-permute-done((f32[264,128]{1,0:T(8,128)S(1)}, f32[264,128]{1,0:T(8,128)S(1)}, u32[]{:S(2)}, u32[]{:S(2)}) %collective-permute-start.24) | collective-permute-done | bytes 135200 | tf_op jit(solution)/shard_map/ppermute | solution.py:41
  98.3 1.8 %collective-permute-start.25 = (f32[264,128]{1,0:T(8,128)S(1)}, f32[264,128]{1,0:T(8,128)S(1)}, u32[]{:S(2)}, u32[]{:S(2)}) collective-permute-start(f32[264,128]{1,0:T(8,128)S(1)} %add.19.p0_ref), channel_id=1, source_target_pairs={{0,64},{64,128},{128,192},{192,0},{1,65},{65,129},{129,193},{193,1... | collective-permute-start | bytes 405512 | tf_op jit(solution)/shard_map/ppermute | solution.py:41
  100.2 2.3 %collective-permute-start.26 = (f32[264,128]{1,0:T(8,128)S(1)}, f32[264,128]{1,0:T(8,128)S(1)}, u32[]{:S(2)}, u32[]{:S(2)}) collective-permute-start(f32[264,128]{1,0:T(8,128)S(1)} %add.19.p0_ref), channel_id=1, source_target_pairs={{0,128},{64,192},{128,0},{192,64},{1,129},{65,193},{129,1},{193,65... | collective-permute-start | bytes 405512 | tf_op jit(solution)/shard_map/ppermute | solution.py:41
  102.4 0.4 collective-permute-start.27
  102.8 0.8 collective-permute-done.25.p1_ref
  103.6 3.6 %collective-permute-done.26.p2_ref = f32[264,128]{1,0:T(8,128)S(1)} collective-permute-done((f32[264,128]{1,0:T(8,128)S(1)}, f32[264,128]{1,0:T(8,128)S(1)}, u32[]{:S(2)}, u32[]{:S(2)}) %collective-permute-start.26) | collective-permute-done | bytes 135200 | tf_op jit(solution)/shard_map/ppermute | solution.py:41
  107.2 0.8 collective-permute-done.27.p3_ref
  108.0 1.4 %place.1 = f32[1024,128]{1,0:T(8,128)} custom-call(s32[5]{0:T(128)S(1)} %stack.19.meta, f32[1024,128]{1,0:T(8,128)S(1)} %copy-done, f32[264,128]{1,0:T(8,128)S(1)} %add.19.p0_ref, f32[264,128]{1,0:T(8,128)S(1)} %collective-permute-done.25.p1_ref, f32[264,128]{1,0:T(8,128)S(1)} %collective-permute-done.26.p2_ref, f32[264,128]{1,0:T(8,128)S(1)} %collective-permute-done.27.p3_ref), custom_call_target="tpu_custom_call" | custom-call | tf_op jit(solution)/shard_map/place/pallas_call | solution.py:240
  (49 shorter events, 2.3 us)
Async XLA Ops:
  1.9 6.7 %collective-permute-start = (bf16[144,128]{1,0:T(8,128)(2,1)S(1)}, bf16[144,128]{1,0:T(8,128)(2,1)S(1)}, u32[]{:S(2)}, u32[]{:S(2)}) collective-permute-start(bf16[144,128]{1,0:T(8,128)(2,1)S(1)} %get-tuple-element.14), channel_id=1, source_target_pairs={{0,2},{2,6},{4,0},{6,4},{1,3},{3,7},{5,1},{7,5},{8,10},{10,14},{12... | collective-permute-start | bytes 110600 | tf_op jit(solution)/shard_map/ppermute | solution.py:41
  4.4 4.6 %collective-permute-start.1 = (bf16[144,128]{1,0:T(8,128)(2,1)S(1)}, bf16[144,128]{1,0:T(8,128)(2,1)S(1)}, u32[]{:S(2)}, u32[]{:S(2)}) collective-permute-start(bf16[144,128]{1,0:T(8,128)(2,1)S(1)} %get-tuple-element.14), channel_id=1, source_target_pairs={{0,6},{2,4},{4,2},{6,0},{1,7},{3,5},{5,3},{7,1},{8,14},{10,12},{12... | collective-permute-start | bytes 110600 | tf_op jit(solution)/shard_map/ppermute | solution.py:41
  7.2 3.1 %collective-permute-start.2 = (bf16[144,128]{1,0:T(8,128)(2,1)S(1)}, bf16[144,128]{1,0:T(8,128)(2,1)S(1)}, u32[]{:S(2)}, u32[]{:S(2)}) collective-permute-start(bf16[144,128]{1,0:T(8,128)(2,1)S(1)} %get-tuple-element.14), channel_id=1, source_target_pairs={{0,4},{2,0},{4,6},{6,2},{1,5},{3,1},{5,7},{7,3},{8,12},{10,8},{12,... | collective-permute-start | bytes 110600 | tf_op jit(solution)/shard_map/ppermute | solution.py:41
  10.3 4.1 %collective-permute-start.3 = (bf16[576,128]{1,0:T(8,128)(2,1)S(1)}, bf16[576,128]{1,0:T(8,128)(2,1)S(1)}, u32[]{:S(2)}, u32[]{:S(2)}) collective-permute-start(bf16[576,128]{1,0:T(8,128)(2,1)S(1)} %get-tuple-element.61), channel_id=1, source_target_pairs={{0,8},{8,0},{16,24},{24,16},{1,9},{9,1},{17,25},{25,17},{2,10},{10... | collective-permute-start | bytes 442376 | tf_op jit(solution)/shard_map/ppermute | solution.py:41
  11.6 7.4 %collective-permute-start.4 = (bf16[576,128]{1,0:T(8,128)(2,1)S(1)}, bf16[576,128]{1,0:T(8,128)(2,1)S(1)}, u32[]{:S(2)}, u32[]{:S(2)}) collective-permute-start(bf16[576,128]{1,0:T(8,128)(2,1)S(1)} %get-tuple-element.61), channel_id=1, source_target_pairs={{0,16},{8,24},{16,0},{24,8},{1,17},{9,25},{17,1},{25,9},{2,18},{10... | collective-permute-start | bytes 442376 | tf_op jit(solution)/shard_map/ppermute | solution.py:41
  14.1 7.6 %collective-permute-start.5 = (bf16[576,128]{1,0:T(8,128)(2,1)S(1)}, bf16[576,128]{1,0:T(8,128)(2,1)S(1)}, u32[]{:S(2)}, u32[]{:S(2)}) collective-permute-start(bf16[576,128]{1,0:T(8,128)(2,1)S(1)} %get-tuple-element.61), channel_id=1, source_target_pairs={{0,24},{8,16},{16,8},{24,0},{1,25},{9,17},{17,9},{25,1},{2,26},{10... | collective-permute-start | bytes 442376 | tf_op jit(solution)/shard_map/ppermute | solution.py:41
  14.4 11.2 %copy-start.2 = (s32[48]{0:T(128)S(1)}, s32[48]{0:T(128)}, u32[]{:S(2)}) copy-start(s32[48]{0:T(128)} %rows.3) | copy-start | bytes 580
  14.4 11.2 %copy-start.3 = (s32[48]{0:T(128)S(1)}, s32[48]{0:T(128)}, u32[]{:S(2)}) copy-start(s32[48]{0:T(128)} %cols.3) | copy-start | bytes 580
  21.7 3.8 %collective-permute-start.6 = (bf16[2304,128]{1,0:T(8,128)(2,1)S(1)}, bf16[2304,128]{1,0:T(8,128)(2,1)S(1)}, u32[]{:S(2)}, u32[]{:S(2)}) collective-permute-start(bf16[2304,128]{1,0:T(8,128)(2,1)S(1)} %get-tuple-element.41), channel_id=1, source_target_pairs={{0,1},{1,0},{2,3},{3,2},{4,5},{5,4},{6,7},{7,6},{8,9},{9,8},{10,11... | collective-permute-start | bytes 1769480 | tf_op jit(solution)/shard_map/ppermute | solution.py:41
  25.6 46.0 %slice-start = ((s8[6291456]{0:T(1024)(128)(4,1)}), s8[4194304]{0:T(1024)(128)(4,1)S(1)}, s32[]{:S(2)}) async-start(s8[6291456]{0:T(1024)(128)(4,1)} %bitcast.4), calls=%async_computation | async-start | bytes 8388608
  29.8 3.5 %collective-permute-start.7 = (bf16[2048,128]{1,0:T(8,128)(2,1)S(1)}, bf16[2048,128]{1,0:T(8,128)(2,1)S(1)}, u32[]{:S(2)}, u32[]{:S(2)}) collective-permute-start(bf16[2048,128]{1,0:T(8,128)(2,1)S(1)} %get-tuple-element.17), channel_id=1, source_target_pairs={{0,1},{1,0},{2,3},{3,2},{4,5},{5,4},{6,7},{7,6},{8,9},{9,8},{10,11... | collective-permute-start | bytes 1572872 | tf_op jit(solution)/shard_map/ppermute | solution.py:41
  33.3 38.4 %slice-start.1 = ((s8[6291456]{0:T(1024)(128)(4,1)}), s8[2097152]{0:T(1024)(128)(4,1)S(1)}, s32[]{:S(2)}) async-start(s8[6291456]{0:T(1024)(128)(4,1)} %bitcast.4), calls=%async_computation.1 | async-start | bytes 4194304
  33.4 17.0 %copy-start.1 = (f32[128,128]{1,0:T(8,128)S(1)}, f32[128,128]{1,0:T(8,128)}, u32[]{:S(2)}) copy-start(f32[128,128]{1,0:T(8,128)} %cell_ref.3) | copy-start | bytes 196612
  33.4 6.0 %collective-permute-start.10 = (bf16[512,128]{1,0:T(8,128)(2,1)S(1)}, bf16[512,128]{1,0:T(8,128)(2,1)S(1)}, u32[]{:S(2)}, u32[]{:S(2)}) collective-permute-start(bf16[512,128]{1,0:T(8,128)(2,1)S(1)} %get-tuple-element.29), channel_id=1, source_target_pairs={{0,24},{8,16},{16,8},{24,0},{1,25},{9,17},{17,9},{25,1},{2,26},{10... | collective-permute-start | bytes 393224 | tf_op jit(solution)/shard_map/ppermute | solution.py:41
  33.5 5.9 %collective-permute-start.8 = (bf16[512,128]{1,0:T(8,128)(2,1)S(1)}, bf16[512,128]{1,0:T(8,128)(2,1)S(1)}, u32[]{:S(2)}, u32[]{:S(2)}) collective-permute-start(bf16[512,128]{1,0:T(8,128)(2,1)S(1)} %get-tuple-element.28), channel_id=1, source_target_pairs={{0,8},{8,0},{16,24},{24,16},{1,9},{9,1},{17,25},{25,17},{2,10},{10... | collective-permute-start | bytes 393224 | tf_op jit(solution)/shard_map/ppermute | solution.py:41
  33.6 9.5 %collective-permute-start.9 = (bf16[512,128]{1,0:T(8,128)(2,1)S(1)}, bf16[512,128]{1,0:T(8,128)(2,1)S(1)}, u32[]{:S(2)}, u32[]{:S(2)}) collective-permute-start(bf16[512,128]{1,0:T(8,128)(2,1)S(1)} %get-tuple-element.30), channel_id=1, source_target_pairs={{0,16},{8,24},{16,0},{24,8},{1,17},{9,25},{17,1},{25,9},{2,18},{10... | collective-permute-start | bytes 393224 | tf_op jit(solution)/shard_map/ppermute | solution.py:41
  43.2 4.1 %collective-permute-start.11 = (f32[128,128]{1,0:T(8,128)S(1)}, f32[128,128]{1,0:T(8,128)S(1)}, u32[]{:S(2)}, u32[]{:S(2)}) collective-permute-start(f32[128,128]{1,0:T(8,128)S(1)} %get-tuple-element.33), channel_id=1, source_target_pairs={{0,2},{2,6},{4,0},{6,4},{1,3},{3,7},{5,1},{7,5},{8,10},{10,14},{12... | collective-permute-start | bytes 196616 | tf_op jit(solution)/shard_map/ppermute | solution.py:41
  44.0 5.1 %collective-permute-start.12 = (f32[128,128]{1,0:T(8,128)S(1)}, f32[128,128]{1,0:T(8,128)S(1)}, u32[]{:S(2)}, u32[]{:S(2)}) collective-permute-start(f32[128,128]{1,0:T(8,128)S(1)} %get-tuple-element.32), channel_id=1, source_target_pairs={{0,6},{2,4},{4,2},{6,0},{1,7},{3,5},{5,3},{7,1},{8,14},{10,12},{12... | collective-permute-start | bytes 196616 | tf_op jit(solution)/shard_map/ppermute | solution.py:41
  46.7 3.7 %collective-permute-start.13 = (f32[128,128]{1,0:T(8,128)S(1)}, f32[128,128]{1,0:T(8,128)S(1)}, u32[]{:S(2)}, u32[]{:S(2)}) collective-permute-start(f32[128,128]{1,0:T(8,128)S(1)} %get-tuple-element.31), channel_id=1, source_target_pairs={{0,4},{2,0},{4,6},{6,2},{1,5},{3,1},{5,7},{7,3},{8,12},{10,8},{12,... | collective-permute-start | bytes 196616 | tf_op jit(solution)/shard_map/ppermute | solution.py:41
  50.5 3.8 %collective-permute-start.14 = (bf16[144,128]{1,0:T(8,128)(2,1)S(1)}, bf16[144,128]{1,0:T(8,128)(2,1)S(1)}, u32[]{:S(2)}, u32[]{:S(2)}) collective-permute-start(bf16[144,128]{1,0:T(8,128)(2,1)S(1)} %get-tuple-element.19), channel_id=1, source_target_pairs={{0,2},{2,6},{4,0},{6,4},{1,3},{3,7},{5,1},{7,5},{8,10},{10,14},{12... | collective-permute-start | bytes 110600 | tf_op jit(solution)/shard_map/ppermute | solution.py:41
  50.6 4.9 %collective-permute-start.15 = (bf16[144,128]{1,0:T(8,128)(2,1)S(1)}, bf16[144,128]{1,0:T(8,128)(2,1)S(1)}, u32[]{:S(2)}, u32[]{:S(2)}) collective-permute-start(bf16[144,128]{1,0:T(8,128)(2,1)S(1)} %get-tuple-element.19), channel_id=1, source_target_pairs={{0,6},{2,4},{4,2},{6,0},{1,7},{3,5},{5,3},{7,1},{8,14},{10,12},{12... | collective-permute-start | bytes 110600 | tf_op jit(solution)/shard_map/ppermute | solution.py:41
  53.1 2.8 %collective-permute-start.16 = (bf16[144,128]{1,0:T(8,128)(2,1)S(1)}, bf16[144,128]{1,0:T(8,128)(2,1)S(1)}, u32[]{:S(2)}, u32[]{:S(2)}) collective-permute-start(bf16[144,128]{1,0:T(8,128)(2,1)S(1)} %get-tuple-element.19), channel_id=1, source_target_pairs={{0,4},{2,0},{4,6},{6,2},{1,5},{3,1},{5,7},{7,3},{8,12},{10,8},{12,... | collective-permute-start | bytes 110600 | tf_op jit(solution)/shard_map/ppermute | solution.py:41
  56.0 4.1 %collective-permute-start.17 = (bf16[576,128]{1,0:T(8,128)(2,1)S(1)}, bf16[576,128]{1,0:T(8,128)(2,1)S(1)}, u32[]{:S(2)}, u32[]{:S(2)}) collective-permute-start(bf16[576,128]{1,0:T(8,128)(2,1)S(1)} %get-tuple-element.49), channel_id=1, source_target_pairs={{0,8},{8,0},{16,24},{24,16},{1,9},{9,1},{17,25},{25,17},{2,10},{10... | collective-permute-start | bytes 442376 | tf_op jit(solution)/shard_map/ppermute | solution.py:41
  56.1 6.7 %collective-permute-start.18 = (bf16[576,128]{1,0:T(8,128)(2,1)S(1)}, bf16[576,128]{1,0:T(8,128)(2,1)S(1)}, u32[]{:S(2)}, u32[]{:S(2)}) collective-permute-start(bf16[576,128]{1,0:T(8,128)(2,1)S(1)} %get-tuple-element.49), channel_id=1, source_target_pairs={{0,16},{8,24},{16,0},{24,8},{1,17},{9,25},{17,1},{25,9},{2,18},{10... | collective-permute-start | bytes 442376 | tf_op jit(solution)/shard_map/ppermute | solution.py:41
  58.6 5.7 %collective-permute-start.19 = (bf16[576,128]{1,0:T(8,128)(2,1)S(1)}, bf16[576,128]{1,0:T(8,128)(2,1)S(1)}, u32[]{:S(2)}, u32[]{:S(2)}) collective-permute-start(bf16[576,128]{1,0:T(8,128)(2,1)S(1)} %get-tuple-element.49), channel_id=1, source_target_pairs={{0,24},{8,16},{16,8},{24,0},{1,25},{9,17},{17,9},{25,1},{2,26},{10... | collective-permute-start | bytes 442376 | tf_op jit(solution)/shard_map/ppermute | solution.py:41
  64.3 7.2 %collective-permute-start.20 = (bf16[2304,128]{1,0:T(8,128)(2,1)S(1)}, bf16[2304,128]{1,0:T(8,128)(2,1)S(1)}, u32[]{:S(2)}, u32[]{:S(2)}) collective-permute-start(bf16[2304,128]{1,0:T(8,128)(2,1)S(1)} %get-tuple-element.35), channel_id=1, source_target_pairs={{0,1},{1,0},{2,3},{3,2},{4,5},{5,4},{6,7},{7,6},{8,9},{9,8},{10,11... | collective-permute-start | bytes 1769480 | tf_op jit(solution)/shard_map/ppermute | solution.py:41
  74.1 34.0 %copy-start = (f32[1024,128]{1,0:T(8,128)S(1)}, f32[1024,128]{1,0:T(8,128)}, u32[]{:S(2)}) copy-start(f32[1024,128]{1,0:T(8,128)} %gene_ref.3) | copy-start | bytes 1572868
  74.1 8.9 %collective-permute-start.21 = (f32[264,128]{1,0:T(8,128)S(1)}, f32[264,128]{1,0:T(8,128)S(1)}, u32[]{:S(2)}, u32[]{:S(2)}) collective-permute-start(f32[264,128]{1,0:T(8,128)S(1)} %get-tuple-element.23), channel_id=1, source_target_pairs={{0,64},{64,128},{128,192},{192,0},{1,65},{65,129},{129,193},{193,1... | collective-permute-start | bytes 405512 | tf_op jit(solution)/shard_map/ppermute | solution.py:41
  79.9 5.9 %collective-permute-start.22 = (f32[264,128]{1,0:T(8,128)S(1)}, f32[264,128]{1,0:T(8,128)S(1)}, u32[]{:S(2)}, u32[]{:S(2)}) collective-permute-start(f32[264,128]{1,0:T(8,128)S(1)} %get-tuple-element.24), channel_id=1, source_target_pairs={{0,128},{64,192},{128,0},{192,64},{1,129},{65,193},{129,1},{193,65... | collective-permute-start | bytes 405512 | tf_op jit(solution)/shard_map/ppermute | solution.py:41
  79.9 6.9 %collective-permute-start.23 = (f32[264,128]{1,0:T(8,128)S(1)}, f32[264,128]{1,0:T(8,128)S(1)}, u32[]{:S(2)}, u32[]{:S(2)}) collective-permute-start(f32[264,128]{1,0:T(8,128)S(1)} %get-tuple-element.25), channel_id=1, source_target_pairs={{0,192},{64,0},{128,64},{192,128},{1,193},{65,1},{129,65},{193,129... | collective-permute-start | bytes 405512 | tf_op jit(solution)/shard_map/ppermute | solution.py:41
  86.8 11.5 %collective-permute-start.24 = (f32[264,128]{1,0:T(8,128)S(1)}, f32[264,128]{1,0:T(8,128)S(1)}, u32[]{:S(2)}, u32[]{:S(2)}) collective-permute-start(f32[264,128]{1,0:T(8,128)S(1)} %fold.1), channel_id=1, source_target_pairs={{0,32},{32,0},{1,33},{33,1},{2,34},{34,2},{3,35},{35,3},{4,36},{36... | collective-permute-start | bytes 405512 | tf_op jit(solution)/shard_map/ppermute | solution.py:41
  98.3 5.3 %collective-permute-start.25 = (f32[264,128]{1,0:T(8,128)S(1)}, f32[264,128]{1,0:T(8,128)S(1)}, u32[]{:S(2)}, u32[]{:S(2)}) collective-permute-start(f32[264,128]{1,0:T(8,128)S(1)} %add.19.p0_ref), channel_id=1, source_target_pairs={{0,64},{64,128},{128,192},{192,0},{1,65},{65,129},{129,193},{193,1... | collective-permute-start | bytes 405512 | tf_op jit(solution)/shard_map/ppermute | solution.py:41
  100.2 7.1 %collective-permute-start.26 = (f32[264,128]{1,0:T(8,128)S(1)}, f32[264,128]{1,0:T(8,128)S(1)}, u32[]{:S(2)}, u32[]{:S(2)}) collective-permute-start(f32[264,128]{1,0:T(8,128)S(1)} %add.19.p0_ref), channel_id=1, source_target_pairs={{0,128},{64,192},{128,0},{192,64},{1,129},{65,193},{129,1},{193,65... | collective-permute-start | bytes 405512 | tf_op jit(solution)/shard_map/ppermute | solution.py:41
  102.4 5.6 %collective-permute-start.27 = (f32[264,128]{1,0:T(8,128)S(1)}, f32[264,128]{1,0:T(8,128)S(1)}, u32[]{:S(2)}, u32[]{:S(2)}) collective-permute-start(f32[264,128]{1,0:T(8,128)S(1)} %add.19.p0_ref), channel_id=1, source_target_pairs={{0,192},{64,0},{128,64},{192,128},{1,193},{65,1},{129,65},{193,129... | collective-permute-start | bytes 405512 | tf_op jit(solution)/shard_map/ppermute | solution.py:41
